TPU v7x, 256 devices: a whole 4x4x8 slice. The times are simulated.
256 devices in a mesh: pipe: 2 (over y_lo), patch: 16 (over x, y_hi, core), hour: 8 (over z).
Axes of the slice: x: 4, y: 4 (y_hi: 2, y_lo: 2; y = y_hi * 2 + y_lo), z: 8, core: 2. Of those that a mesh axis runs over, the one named last changes fastest.
Arguments:
- inputs: bfloat16 [2, 256, 128, 512], P(None, 'patch', 'hour'), may hold values from -6 to 6
- visibility: int32 [4, 2], replicated, may hold values from 0 to 3, all different within a row
- norm_gains: float32 [2, 3, 512], P('pipe'), may hold values from 0.1 to 1.9
- scales: float32 [2, 2, 8], P('pipe'), may hold values from 2 to 12
- mixer_in: bfloat16 [2, 2, 512, 1536], P('pipe'), may hold values from -0.25 to 0.25
- mixer_out: bfloat16 [2, 2, 512, 512], P('pipe'), may hold values from -0.25 to 0.25
- expand_weight: bfloat16 [2, 512, 2048], P('pipe'), may hold values from -0.25 to 0.25
- reduce_weight: bfloat16 [2, 2048, 512], P('pipe'), may hold values from -0.125 to 0.125
Outputs:
- outputs: bfloat16 [2, 256, 128, 512], P(None, 'patch', 'hour')
Inputs may be any that keep to these rules, and one draw needn't show every extreme that they name: `visibility`: row b lists 2 different key blocks of 64 patches for query block b; every block is listed in some row.
All inputs are finite; a program needn't handle non-finite values.
Results may differ from a plain program's by a relative error of at most 0.023.
Values may be sent and summed in bfloat16 or wider, within the bound.
A program may use at most 64 MiB of HBM per device.

v0:
```python
import jax
import jax.numpy as jnp
from jax import lax
from jax.sharding import PartitionSpec as P

HEADS = 8
HEAD_DIM = 64
PB = 64
KV = 2


def shifted(value, axis, steps):
    count = lax.axis_size(axis)
    pairs = [(source, (source + steps) % count) for source in range(count)]
    return lax.ppermute(value, axis, pairs)


def rms_norm(values, gain):
    values = values.astype(jnp.float32)
    factor = lax.rsqrt(jnp.mean(values * values, axis=-1, keepdims=True) + 1e-05)
    return (values * factor * gain).astype(jnp.bfloat16)


def head_norm(values):
    factor = lax.rsqrt(jnp.mean(values * values, axis=-1, keepdims=True) + 1e-06)
    return (values * factor).astype(jnp.bfloat16)


def split_heads(projected, lead_shape):
    width = projected.shape[-1] // 3
    shape = lead_shape + (HEADS, HEAD_DIM)
    queries = head_norm(projected[:, :width].reshape(shape))
    keys_all = head_norm(projected[:, width : 2 * width].reshape(shape))
    values = projected[:, 2 * width :].astype(jnp.bfloat16).reshape(shape)
    return (queries, keys_all, values)


def softmax_weights(scores, scale):
    scaled = scores * (scale / HEAD_DIM)[:, None, None]
    powers = jnp.exp(scaled)
    return (powers / jnp.sum(powers, axis=-1, keepdims=True)).astype(jnp.bfloat16)


def time_mix(tokens, gain, weight_in, weight_out, scale):
    count_p, count_h, width = tokens.shape
    normed = rms_norm(tokens, gain).reshape(-1, width)
    projected = jnp.dot(normed, weight_in, preferred_element_type=jnp.float32)
    queries, keys_all, values = split_heads(projected, (count_p, count_h))
    scores = jnp.einsum("pqnd,pknd->pnqk", queries, keys_all, preferred_element_type=jnp.float32)
    weights = softmax_weights(scores, scale)
    attended = jnp.einsum("pnqk,pknd->pqnd", weights, values, preferred_element_type=jnp.float32)
    attended = attended.astype(jnp.bfloat16).reshape(-1, width)
    update = jnp.dot(attended, weight_out, preferred_element_type=jnp.float32)
    return (tokens.astype(jnp.float32) + update.reshape(tokens.shape)).astype(jnp.bfloat16)


def patch_mix(tokens, visibility, gain, weight_in, weight_out, scale):
    count_p, count_h, width = tokens.shape
    blocks = count_p // PB
    normed = rms_norm(tokens, gain).reshape(-1, width)
    projected = jnp.dot(normed, weight_in, preferred_element_type=jnp.float32)
    queries, keys_all, values = split_heads(projected, (count_p, count_h))
    block_shape = (blocks, PB, count_h, HEADS, HEAD_DIM)
    seen_shape = (blocks, KV * PB, count_h, HEADS, HEAD_DIM)
    query_blocks = queries.reshape(block_shape)
    key_blocks = jnp.take(keys_all.reshape(block_shape), visibility, axis=0).reshape(seen_shape)
    value_blocks = jnp.take(values.reshape(block_shape), visibility, axis=0).reshape(seen_shape)
    scores = jnp.einsum(
        "bqtnd,bktnd->btnqk", query_blocks, key_blocks, preferred_element_type=jnp.float32
    )
    weights = softmax_weights(scores, scale)
    attended = jnp.einsum(
        "btnqk,bktnd->bqtnd", weights, value_blocks, preferred_element_type=jnp.float32
    )
    attended = attended.astype(jnp.bfloat16).reshape(-1, width)
    update = jnp.dot(attended, weight_out, preferred_element_type=jnp.float32)
    return (tokens.astype(jnp.float32) + update.reshape(tokens.shape)).astype(jnp.bfloat16)


def feed_forward(tokens, gain, weight_up, weight_down):
    width = tokens.shape[-1]
    normed = rms_norm(tokens, gain).reshape(-1, width)
    hidden = jax.nn.gelu(jnp.dot(normed, weight_up, preferred_element_type=jnp.float32)).astype(
        jnp.bfloat16
    )
    update = jnp.dot(hidden, weight_down, preferred_element_type=jnp.float32)
    return (tokens.astype(jnp.float32) + update.reshape(tokens.shape)).astype(jnp.bfloat16)


def run_block(tokens, visibility, gains, scales, mixer_in, mixer_out, expand_weight, reduce_weight):
    hourly = lax.all_to_all(tokens, "hour", split_axis=0, concat_axis=1, tiled=True)
    hourly = time_mix(hourly, gains[0], mixer_in[0], mixer_out[0], scales[0])
    restored = lax.all_to_all(hourly, "hour", split_axis=1, concat_axis=0, tiled=True)
    spread = lax.all_to_all(restored, "patch", split_axis=1, concat_axis=0, tiled=True)
    spread = patch_mix(spread, visibility, gains[1], mixer_in[1], mixer_out[1], scales[1])
    tokens = lax.all_to_all(spread, "patch", split_axis=0, concat_axis=1, tiled=True)
    return feed_forward(tokens, gains[2], expand_weight, reduce_weight)


def local(
    inputs, visibility, norm_gains, scales, mixer_in, mixer_out, expand_weight, reduce_weight
):
    gains = norm_gains[0]
    head_scales = scales[0]
    weights_in = mixer_in[0]
    weights_out = mixer_out[0]
    weight_up = expand_weight[0]
    weight_down = reduce_weight[0]
    leading = lax.axis_index("pipe") == 0
    micro_count = inputs.shape[0]
    arrived = jnp.zeros_like(inputs[0])
    finished = []
    for step_index in range(micro_count + 1):
        supplied = inputs[min(step_index, micro_count - 1)]
        current = jnp.where(leading, supplied, arrived)
        produced = run_block(
            current, visibility, gains, head_scales, weights_in, weights_out, weight_up, weight_down
        )
        arrived = shifted(produced, "pipe", 1)
        if step_index >= 1:
            finished.append(jnp.where(leading, arrived, produced))
    stacked = jnp.stack(finished)
    return stacked


def solution(mesh):
    placed = (
        P(None, "patch", "hour", None),
        P(),
        P("pipe", None, None),
        P("pipe", None, None),
        P("pipe", None, None, None),
        P("pipe", None, None, None),
        P("pipe", None, None),
        P("pipe", None, None),
    )
    return jax.shard_map(
        local, mesh=mesh, in_specs=placed, out_specs=P(None, "patch", "hour", None), check_vma=False
    )
```

profile of v0, /device:TPU:1, one launch (start us, length us, event | category | flops | bytes accessed | tf_op | source)
XLA Modules:
  0.0 446.2 jit_solution(14026854366194232207)
XLA Ops:
  1.8 9.0 %all-to-all-start = ((bf16[16,16,512]{2,1,0:T(8,128)(2,1)}), bf16[16,16,512]{2,1,0:T(8,128)(2,1)S(1)}, u32[]{:S(2)}, u32[]{:S(2)}) async-start(bf16[16,16,512]{2,1,0:T(8,128)(2,1)} %select_bitcast_fusion.2), calls=%async_computation | async-start | bytes 524288 | tf_op jit(solution)/shard_map/all_to_all | solution.py:91
  12.3 8.9 %all-to-all-done = bf16[16,16,512]{2,1,0:T(8,128)(2,1)S(1)} async-done(((bf16[16,16,512]{2,1,0:T(8,128)(2,1)}), bf16[16,16,512]{2,1,0:T(8,128)(2,1)S(1)}, u32[]{:S(2)}, u32[]{:S(2)}) %all-to-all-start) | async-done | bytes 262176 | tf_op jit(solution)/shard_map/all_to_all | solution.py:91
  38.3 3.4 all-to-all-start.1
  41.8 9.2 %all-to-all-done.1 = bf16[2,128,512]{2,0,1:T(2,128)(2,1)S(1)} async-done(((bf16[2,128,512]{2,0,1:T(2,128)(2,1)}), bf16[2,128,512]{2,0,1:T(2,128)(2,1)S(1)}, u32[]{:S(2)}, u32[]{:S(2)}) %all-to-all-start.1) | async-done | bytes 262176 | tf_op jit(solution)/shard_map/all_to_all | solution.py:93
  51.9 10.8 %all-to-all-start.2 = ((bf16[16,16,512]{2,0,1:T(8,128)(2,1)}), bf16[16,16,512]{2,0,1:T(8,128)(2,1)S(1)}, u32[]{:S(2)}, u32[]{:S(2)}) async-start(bf16[16,16,512]{2,0,1:T(8,128)(2,1)} %copy.296), calls=%async_computation.2 | async-start | bytes 524288 | tf_op jit(solution)/shard_map/all_to_all | solution.py:94
  63.0 8.6 %all-to-all-done.2 = bf16[16,16,512]{2,0,1:T(8,128)(2,1)S(1)} async-done(((bf16[16,16,512]{2,0,1:T(8,128)(2,1)}), bf16[16,16,512]{2,0,1:T(8,128)(2,1)S(1)}, u32[]{:S(2)}, u32[]{:S(2)}) %all-to-all-start.2) | async-done | bytes 262176 | tf_op jit(solution)/shard_map/all_to_all | solution.py:94
  76.8 2.8 gather_fusion
  79.6 3.9 copy.301
  92.3 2.4 fusion.99
  94.7 2.8 gather_fusion.1
  97.4 4.0 copy.309
  101.4 4.7 %broadcast_select_fusion.4 = (bf16[4,2,64,1,8,64]{2,1,5,4,0,3:T(2,128)(2,1)}, bf16[4,2,64,1,8,64]{2,1,5,4,0,3:T(2,128)(2,1)}) fusion(bf16[4,2,64,1,8,64]{2,1,5,4,0,3:T(2,128)(2,1)} %copy.309, pred[4,2]{1,0:T(4,128)(4,1)S(1)} %copy.297, bf16[4,2,64,1,8,64]{2,1,5,4,0,3:T(2,128)(2,1)} %copy.301), kind=kLoop, calls=%fused_computation.49 | loop fusion | flops 524288 | bytes 2097160 | tf_op jit(solution)/shard_map/jit(_take)/select_n | solution.py:66
  106.1 3.1 reshape.1081
  109.2 3.1 reshape.1078
  114.6 2.8 fusion.56
  117.4 3.0 fusion.69
  129.0 13.0 %all_to_all.135 = bf16[16,2,4096]{2,1,0:T(2,128)(2,1)S(1)} all-to-all(bf16[16,2,4096]{2,1,0:T(2,128)(2,1)} %reshape.1245), channel_id=1, replica_groups=mesh['pipe'=2,'patch'=16,'hour'=8] {'patch'}, dimensions={0} | all-to-all | bytes 524288 | tf_op jit(solution)/shard_map/all_to_all | solution.py:96
  147.7 7.1 %collective-permute-done = bf16[16,16,512]{2,1,0:T(8,128)(2,1)S(1)} collective-permute-done((bf16[16,16,512]{2,1,0:T(8,128)(2,1)S(1)}, bf16[16,16,512]{2,1,0:T(8,128)(2,1)S(1)}, u32[]{:S(2)}, u32[]{:S(2)}) %collective-permute-start) | collective-permute-done | bytes 262176 | tf_op jit(solution)/shard_map/ppermute | solution.py:15
  154.8 12.5 %all_to_all.136 = bf16[16,16,512]{2,1,0:T(8,128)(2,1)S(1)} all-to-all(bf16[16,16,512]{2,1,0:T(8,128)(2,1)S(1)} %bitcast_select_fusion.1), channel_id=1, replica_groups=mesh['pipe'=2,'patch'=16,'hour'=8] {'hour'}, dimensions={0} | all-to-all | bytes 524288 | tf_op jit(solution)/shard_map/all_to_all | solution.py:91
  190.5 12.1 %all_to_all.137 = bf16[2,128,512]{2,0,1:T(2,128)(2,1)S(1)} all-to-all(bf16[2,128,512]{2,0,1:T(2,128)(2,1)S(1)} %copy.323), channel_id=1, replica_groups=mesh['pipe'=2,'patch'=16,'hour'=8] {'hour'}, dimensions={1} | all-to-all | bytes 524288 | tf_op jit(solution)/shard_map/all_to_all | solution.py:93
  202.8 16.1 %all_to_all.138 = bf16[16,16,512]{2,0,1:T(8,128)(2,1)S(1)} all-to-all(bf16[16,16,512]{2,0,1:T(8,128)(2,1)S(1)} %copy.326), channel_id=1, replica_groups=mesh['pipe'=2,'patch'=16,'hour'=8] {'patch'}, dimensions={1} | all-to-all | bytes 524288 | tf_op jit(solution)/shard_map/all_to_all | solution.py:94
  224.1 2.8 gather_fusion.2
  226.8 3.9 copy.331
  239.6 2.4 fusion.100
  242.0 2.8 gather_fusion.3
  244.7 4.0 copy.339
  248.7 4.7 %broadcast_select_fusion.2 = (bf16[4,2,64,1,8,64]{2,1,5,4,0,3:T(2,128)(2,1)}, bf16[4,2,64,1,8,64]{2,1,5,4,0,3:T(2,128)(2,1)}) fusion(bf16[4,2,64,1,8,64]{2,1,5,4,0,3:T(2,128)(2,1)} %copy.339, pred[4,2]{1,0:T(4,128)(4,1)S(1)} %copy.297, bf16[4,2,64,1,8,64]{2,1,5,4,0,3:T(2,128)(2,1)} %copy.331), kind=kLoop, calls=%fused_computation.47 | loop fusion | flops 524288 | bytes 2097160 | tf_op jit(solution)/shard_map/jit(_take)/select_n | solution.py:66
  253.4 3.1 reshape.1089
  256.5 3.1 reshape.1086
  261.9 2.8 fusion.55
  264.7 3.0 fusion.70
  275.8 12.8 %all_to_all.139 = bf16[16,2,4096]{2,1,0:T(2,128)(2,1)S(1)} all-to-all(bf16[16,2,4096]{2,1,0:T(2,128)(2,1)} %reshape.1247), channel_id=1, replica_groups=mesh['pipe'=2,'patch'=16,'hour'=8] {'patch'}, dimensions={0} | all-to-all | bytes 524288 | tf_op jit(solution)/shard_map/all_to_all | solution.py:96
  294.3 7.1 %collective-permute-done.1 = bf16[16,16,512]{2,1,0:T(8,128)(2,1)S(1)} collective-permute-done((bf16[16,16,512]{2,1,0:T(8,128)(2,1)S(1)}, bf16[16,16,512]{2,1,0:T(8,128)(2,1)S(1)}, u32[]{:S(2)}, u32[]{:S(2)}) %collective-permute-start.1) | collective-permute-done | bytes 262176 | tf_op jit(solution)/shard_map/ppermute | solution.py:15
  302.1 12.5 %all_to_all.140 = bf16[16,16,512]{2,1,0:T(8,128)(2,1)S(1)} all-to-all(bf16[16,16,512]{2,1,0:T(8,128)(2,1)S(1)} %get-tuple-element.25), channel_id=1, replica_groups=mesh['pipe'=2,'patch'=16,'hour'=8] {'hour'}, dimensions={0} | all-to-all | bytes 524288 | tf_op jit(solution)/shard_map/all_to_all | solution.py:91
  337.7 12.1 %all_to_all.141 = bf16[2,128,512]{2,0,1:T(2,128)(2,1)S(1)} all-to-all(bf16[2,128,512]{2,0,1:T(2,128)(2,1)S(1)} %copy.353), channel_id=1, replica_groups=mesh['pipe'=2,'patch'=16,'hour'=8] {'hour'}, dimensions={1} | all-to-all | bytes 524288 | tf_op jit(solution)/shard_map/all_to_all | solution.py:93
  350.1 15.7 %all_to_all.142 = bf16[16,16,512]{2,0,1:T(8,128)(2,1)S(1)} all-to-all(bf16[16,16,512]{2,0,1:T(8,128)(2,1)S(1)} %copy.356), channel_id=1, replica_groups=mesh['pipe'=2,'patch'=16,'hour'=8] {'patch'}, dimensions={1} | all-to-all | bytes 524288 | tf_op jit(solution)/shard_map/all_to_all | solution.py:94
  371.0 2.8 gather_fusion.4
  373.7 3.9 copy.361
  386.5 2.4 fusion.101
  388.9 2.8 gather_fusion.5
  391.6 4.0 copy.369
  395.6 4.7 %broadcast_select_fusion = (bf16[4,2,64,1,8,64]{2,1,5,4,0,3:T(2,128)(2,1)}, bf16[4,2,64,1,8,64]{2,1,5,4,0,3:T(2,128)(2,1)}) fusion(bf16[4,2,64,1,8,64]{2,1,5,4,0,3:T(2,128)(2,1)} %copy.369, pred[4,2]{1,0:T(4,128)(4,1)S(1)} %copy.297, bf16[4,2,64,1,8,64]{2,1,5,4,0,3:T(2,128)(2,1)} %copy.361), kind=kLoop, calls=%fused_computation.45 | loop fusion | flops 524288 | bytes 2097160 | tf_op jit(solution)/shard_map/jit(_take)/select_n | solution.py:66
  400.3 3.1 reshape.1097
  403.4 3.1 reshape.1094
  408.8 2.8 fusion.54
  411.6 3.0 fusion.71
  422.0 12.0 %all_to_all.143 = bf16[16,2,4096]{2,1,0:T(2,128)(2,1)S(1)} all-to-all(bf16[16,2,4096]{2,1,0:T(2,128)(2,1)S(1)} %reshape.1249), channel_id=1, replica_groups=mesh['pipe'=2,'patch'=16,'hour'=8] {'patch'}, dimensions={0} | all-to-all | bytes 524288 | tf_op jit(solution)/shard_map/all_to_all | solution.py:96
  438.0 7.1 %collective-permute-done.2 = bf16[16,16,512]{2,1,0:T(8,128)(2,1)S(1)} collective-permute-done((bf16[16,16,512]{2,1,0:T(8,128)(2,1)S(1)}, bf16[16,16,512]{2,1,0:T(8,128)(2,1)S(1)}, u32[]{:S(2)}, u32[]{:S(2)}) %collective-permute-start.2) | collective-permute-done | bytes 262176 | tf_op jit(solution)/shard_map/ppermute | solution.py:15
  (225 shorter events, 157.4 us)
Async XLA Ops:
  0.0 144.7 %copy-start = (bf16[1,512,2048]{2,1,0:T(8,128)(2,1)S(1)}, bf16[1,512,2048]{2,1,0:T(8,128)(2,1)}, u32[]{:S(2)}) copy-start(bf16[1,512,2048]{2,1,0:T(8,128)(2,1)} %param.16) | copy-start | bytes 6291460
  1.8 19.4 %all-to-all-start = ((bf16[16,16,512]{2,1,0:T(8,128)(2,1)}), bf16[16,16,512]{2,1,0:T(8,128)(2,1)S(1)}, u32[]{:S(2)}, u32[]{:S(2)}) async-start(bf16[16,16,512]{2,1,0:T(8,128)(2,1)} %select_bitcast_fusion.2), calls=%async_computation | async-start | bytes 524288 | tf_op jit(solution)/shard_map/all_to_all | solution.py:91
  33.8 2.1 copy-start.3
  35.9 5.8 %copy-start.12 = (s32[4,2]{0,1:T(2,128)S(1)}, s32[4,2]{0,1:T(2,128)}, u32[]{:S(2)}) copy-start(s32[4,2]{0,1:T(2,128)} %param.11) | copy-start | bytes 100
  38.3 12.8 %all-to-all-start.1 = ((bf16[2,128,512]{2,0,1:T(2,128)(2,1)}), bf16[2,128,512]{2,0,1:T(2,128)(2,1)S(1)}, u32[]{:S(2)}, u32[]{:S(2)}) async-start(bf16[2,128,512]{2,0,1:T(2,128)(2,1)} %copy.293), calls=%async_computation.1 | async-start | bytes 524288 | tf_op jit(solution)/shard_map/all_to_all | solution.py:93
  51.9 19.6 %all-to-all-start.2 = ((bf16[16,16,512]{2,0,1:T(8,128)(2,1)}), bf16[16,16,512]{2,0,1:T(8,128)(2,1)S(1)}, u32[]{:S(2)}, u32[]{:S(2)}) async-start(bf16[16,16,512]{2,0,1:T(8,128)(2,1)} %copy.296), calls=%async_computation.2 | async-start | bytes 524288 | tf_op jit(solution)/shard_map/all_to_all | solution.py:94
  72.0 2.3 copy-start.5
  144.8 1.6 copy-start.13
  145.8 9.0 %copy-start.7 = (bf16[2,16,16,512]{3,2,1,0:T(8,128)(2,1)S(1)}, bf16[2,16,16,512]{3,2,1,0:T(8,128)(2,1)}, u32[]{:S(2)}) copy-start(bf16[2,16,16,512]{3,2,1,0:T(8,128)(2,1)} %param.10) | copy-start | bytes 1572868
  147.2 20.4 %copy-start.1 = (bf16[1,2,512,1536]{3,2,1,0:T(8,128)(2,1)S(1)}, bf16[1,2,512,1536]{3,2,1,0:T(8,128)(2,1)}, u32[]{:S(2)}) copy-start(bf16[1,2,512,1536]{3,2,1,0:T(8,128)(2,1)} %param.14) | copy-start | bytes 9437188
  147.2 7.5 %collective-permute-start = (bf16[16,16,512]{2,1,0:T(8,128)(2,1)S(1)}, bf16[16,16,512]{2,1,0:T(8,128)(2,1)S(1)}, u32[]{:S(2)}, u32[]{:S(2)}) collective-permute-start(bf16[16,16,512]{2,1,0:T(8,128)(2,1)S(1)} %fusion.78), channel_id=1, source_target_pairs={{0,128},{128,0},{1,129},{129,1},{2,130},{130,2},{3,131},{131,3},{4... | collective-permute-start | bytes 786440 | tf_op jit(solution)/shard_map/ppermute | solution.py:15
  178.7 6.7 %copy-start.11 = (bf16[2,128,8,64]{1,0,3,2:T(2,128)(2,1)S(1)}, bf16[2,128,8,64]{1,0,3,2:T(2,128)(2,1)}, u32[]{:S(2)}) copy-start(bf16[2,128,8,64]{1,0,3,2:T(2,128)(2,1)} %multiply_convert_fusion.8) | copy-start | bytes 786436
  219.3 2.3 copy-start.6
  291.3 1.6 copy-start.14
  292.4 9.0 %copy-start.8 = (bf16[2,16,16,512]{3,2,1,0:T(8,128)(2,1)S(1)}, bf16[2,16,16,512]{3,2,1,0:T(8,128)(2,1)}, u32[]{:S(2)}) copy-start(bf16[2,16,16,512]{3,2,1,0:T(8,128)(2,1)} %param.10) | copy-start | bytes 1572868
  293.8 21.1 %copy-start.2 = (bf16[1,2,512,1536]{3,2,1,0:T(8,128)(2,1)S(1)}, bf16[1,2,512,1536]{3,2,1,0:T(8,128)(2,1)}, u32[]{:S(2)}) copy-start(bf16[1,2,512,1536]{3,2,1,0:T(8,128)(2,1)} %param.14) | copy-start | bytes 9437188
  293.8 7.5 %collective-permute-start.1 = (bf16[16,16,512]{2,1,0:T(8,128)(2,1)S(1)}, bf16[16,16,512]{2,1,0:T(8,128)(2,1)S(1)}, u32[]{:S(2)}, u32[]{:S(2)}) collective-permute-start(bf16[16,16,512]{2,1,0:T(8,128)(2,1)S(1)} %fusion.75), channel_id=1, source_target_pairs={{0,128},{128,0},{1,129},{129,1},{2,130},{130,2},{3,131},{131,3},{4... | collective-permute-start | bytes 786440 | tf_op jit(solution)/shard_map/ppermute | solution.py:15
  326.0 6.7 %copy-start.10 = (bf16[2,128,8,64]{1,0,3,2:T(2,128)(2,1)S(1)}, bf16[2,128,8,64]{1,0,3,2:T(2,128)(2,1)}, u32[]{:S(2)}) copy-start(bf16[2,128,8,64]{1,0,3,2:T(2,128)(2,1)} %multiply_convert_fusion.5) | copy-start | bytes 786436
  366.2 2.3 copy-start.4
  435.0 1.6 copy-start.15
  436.6 8.5 %copy-start.9 = (bf16[1,16,16,512]{3,2,1,0:T(8,128)(2,1)S(1)}, bf16[1,16,16,512]{3,2,1,0:T(8,128)(2,1)}, u32[]{:S(2)}) copy-start(bf16[1,16,16,512]{3,2,1,0:T(8,128)(2,1)} %get-tuple-element.24) | copy-start | bytes 786436
  437.5 7.6 %collective-permute-start.2 = (bf16[16,16,512]{2,1,0:T(8,128)(2,1)S(1)}, bf16[16,16,512]{2,1,0:T(8,128)(2,1)S(1)}, u32[]{:S(2)}, u32[]{:S(2)}) collective-permute-start(bf16[16,16,512]{2,1,0:T(8,128)(2,1)S(1)} %fusion.72), channel_id=1, source_target_pairs={{0,128},{128,0},{1,129},{129,1},{2,130},{130,2},{3,131},{131,3},{4... | collective-permute-start | bytes 786440 | tf_op jit(solution)/shard_map/ppermute | solution.py:15
where the time goes:
time: 455 us; the launch traced here: 446 us
  local copies, waits for them, and re-layouts  141 us (31%)
  blocking collectives  119 us (26%)
  other arithmetic  59.4 us (13%)
  matrix products  53.5 us (12%)
  waiting for transfers between devices  47.9 us (11%)
  starting transfers between devices  24.7 us (5%)
    all_to_all x3, blocking collectives, run_block(): lax.all_to_all(spread, 'patch', split_axis=0, concat_axis=1, tiled=True)  37.8 us
    all_to_all x2, blocking collectives, run_block(): lax.all_to_all(restored, 'patch', split_axis=1, concat_axis=0, tiled=True)  31.8 us
    all_to_all x2, blocking collectives, run_block(): lax.all_to_all(tokens, 'hour', split_axis=0, concat_axis=1, tiled=True)  25 us
    all_to_all x2, blocking collectives, run_block(): lax.all_to_all(hourly, 'hour', split_axis=1, concat_axis=0, tiled=True)  24.2 us
    ppermute x3, waiting for transfers between devices, shifted(): return lax.ppermute(value, axis, pairs)  21.2 us
    gather x6, local copies, waits for them, and re-layouts, patch_mix(): jnp.take(keys_all.reshape(block_shape), visibility, axis=0)  20.1 us
    gather x6, local copies, waits for them, and re-layouts, patch_mix(): jnp.take(values.reshape(block_shape), visibility, axis=0)  20 us
    another operation x6, local copies, waits for them, and re-layouts  18.5 us
  transfers between devices with their start and end apart: 6, of which 6 were waited for; matrix products, arithmetic and copies ran while one was open for 0% of the time, Pallas kernels for 0%

commit v1 on v0

v1 whole, which is shorter than its diff:
```python
import functools
import math

import jax
import jax.numpy as jnp
from jax import lax
from jax.experimental import pallas as pl
from jax.experimental.pallas import tpu as pltpu
from jax.sharding import PartitionSpec as P

HEADS = 8
HEAD_DIM = 64
PB = 64
KV = 2
BF = jnp.bfloat16
F32 = jnp.float32
MESH = pl.DeviceIdType.MESH


def iota(shape, axis):
    return lax.broadcasted_iota(jnp.int32, shape, axis)


def dot(a, b):
    return jnp.dot(a, b, preferred_element_type=F32)


def dot_nt(a, b):
    return lax.dot_general(a, b, (((1,), (1,)), ((), ())), preferred_element_type=F32)


def rms(x, gain):
    x = x.astype(F32)
    factor = lax.rsqrt(jnp.mean(x * x, axis=-1, keepdims=True) + 1e-05)
    return (x * factor * gain).astype(BF)


def fill_constants(turn, same_head, pair_sums):
    r, c = iota((256, 256), 0), iota((256, 256), 1)
    turn[...] = jnp.where(c == (r % 16) * 16 + r // 16, 1.0, 0.0).astype(BF)
    same_head[...] = jnp.where(r // HEAD_DIM == c // HEAD_DIM, 1.0, 0.0).astype(BF)
    r, c = iota((256, 128), 0), iota((256, 128), 1)
    pair_sums[...] = jnp.where(r // 128 == c // HEAD_DIM, 1.0, 0.0).astype(BF)


def project(normed, which, weight_in, scales, same_head, q_s, ke_s, ko_s, ve_s, vo_s):
    width = 2 * 256
    lane = iota((1, 256), 1)
    even = (lane // HEAD_DIM) % 2 == 0
    zero = jnp.zeros((256, 256), BF)
    for part in range(3):
        for half in range(2):
            at = pl.ds(half * 256, 256)
            value = dot(normed, weight_in[which, :, pl.ds(part * width + half * 256, 256)])
            if part < 2:
                squares = dot((value * value).astype(BF), same_head[...])
                value = value * lax.rsqrt(squares * (1.0 / HEAD_DIM) + 1e-06)
            if part == 0:
                row = jnp.zeros((1, 256), F32)
                for n in range(4):
                    scale = scales[0, which, half * 4 + n] * (math.log2(math.e) / HEAD_DIM)
                    row = jnp.where(lane // HEAD_DIM == n, scale, row)
                q_s[:, at] = (value * row).astype(BF)
            else:
                even_s, odd_s = (ke_s, ko_s) if part == 1 else (ve_s, vo_s)
                value = value.astype(BF)
                even_s[:, :, at] = jnp.where(even, value, zero).reshape(4, PB, 256)
                odd_s[:, :, at] = jnp.where(even, zero, value).reshape(4, PB, 256)


def attend(queries, keys, values, pair_sums):
    weights = jnp.exp2(dot_nt(queries, keys)).astype(BF)
    mixed = dot(weights, jnp.concatenate([values, pair_sums], axis=1))
    return (mixed[:, :128] / mixed[:, 128:]).astype(BF)


def gelu(u):
    return 0.5 * u * (1.0 + jnp.tanh(math.sqrt(2.0 / math.pi) * (u + 0.044715 * (u * u * u))))


def time_stage(x, gains, scales, w_in, w_out, same_head, pair_sums, q_s, ke_s, ko_s, ve_s, vo_s, att_s):
    normed = rms(x, gains[0, 0:1, :])
    project(normed, 0, w_in, scales, same_head, q_s, ke_s, ko_s, ve_s, vo_s)
    for a in range(2):
        rows = pl.ds(a * 128, 128)
        for j in range(4):
            at = pl.ds(j * 128, 128)
            keys = jnp.concatenate([k[2 * a + i, :, at] for k in (ke_s, ko_s) for i in range(2)], axis=0)
            values = jnp.concatenate([v[2 * a + i, :, at] for v in (ve_s, vo_s) for i in range(2)], axis=0)
            att_s[rows, at] = attend(q_s[rows, at], keys, values, pair_sums[...])
    return (x.astype(F32) + dot(att_s[...], w_out[0])).astype(BF)


def patch_stage(
    x, vis, gains, scales, w_in, w_out, same_head, pair_sums, q_s, ke_s, ko_s, ve_s, vo_s, att_s
):
    normed = rms(x, gains[0, 1:2, :])
    project(normed, 1, w_in, scales, same_head, q_s, ke_s, ko_s, ve_s, vo_s)
    for b in range(4):
        rows = pl.ds(b * PB, PB)
        seen = [vis[b, i] for i in range(KV)]
        for j in range(4):
            at = pl.ds(j * 128, 128)
            keys = jnp.concatenate([s[z, :, at] for s in (ke_s, ko_s) for z in seen], axis=0)
            values = jnp.concatenate([s[z, :, at] for s in (ve_s, vo_s) for z in seen], axis=0)
            att_s[rows, at] = attend(q_s[rows, at], keys, values, pair_sums[...])
    return (x.astype(F32) + dot(att_s[...], w_out[1])).astype(BF)


def feed_forward(x, gains, up, down, hidden):
    normed = rms(x, gains[0, 2:3, :])
    for c in range(8):
        at = pl.ds(c * 256, 256)
        hidden[:, at] = gelu(dot(normed, up[:, at])).astype(BF)
    return (x.astype(F32) + dot(hidden[...], down[...])).astype(BF)


def loop(start, stop, body):
    def step(i, carry):
        body(i)
        return carry

    lax.fori_loop(start, stop, step, 0)


def kernel(
    n_patch,
    n_hour,
    vis,
    scales,
    gains,
    inputs,
    w_in_hbm,
    w_out_hbm,
    up_hbm,
    down_hbm,
    out,
    w_in,
    w_out,
    up,
    down,
    timed,
    mixed,
    homed,
    turned,
    spread,
    result,
    back,
    handed,
    final,
    turn,
    same_head,
    pair_sums,
    q_s,
    ke_s,
    ko_s,
    ve_s,
    vo_s,
    att_s,
    hidden,
    w_sem,
    timed_sem,
    homed_sem,
    spread_sem,
    back_sem,
    out_sem,
    in_send,
    mixed_send,
    turned_send,
    result_send,
    final_send,
    handed_send,
):
    s = lax.axis_index("pipe")
    p = lax.axis_index("patch")
    h = lax.axis_index("hour")

    loads = [
        pltpu.make_async_copy(src.at[0], dst, w_sem.at[i])
        for i, (src, dst) in enumerate(
            [(w_in_hbm, w_in), (w_out_hbm, w_out), (up_hbm, up), (down_hbm, down)]
        )
    ]
    for load in loads:
        load.start()

    def at16(i):
        return pl.ds(pl.multiple_of(i * 16, 16), 16)

    def remote(src, dst, send, recv, device):
        pltpu.make_async_remote_copy(
            src_ref=src,
            dst_ref=dst,
            send_sem=send,
            recv_sem=recv,
            device_id=device,
            device_id_type=MESH,
        ).start()

    def arrive(ref, sem):
        pltpu.make_async_copy(ref, ref, sem).wait()

    barrier = pltpu.get_barrier_semaphore()

    def greet(device):
        pl.semaphore_signal(barrier, inc=1, device_id=device, device_id_type=MESH)

    loop(1, n_hour, lambda k: greet((s, p, lax.rem(h + k, n_hour))))
    loop(1, n_patch, lambda k: greet((s, lax.rem(p + k, n_patch), h)))

    @pl.when(s == 0)
    def _():
        loop(0, n_patch, lambda k: greet((1, k, h)))

    @pl.when(s == 1)
    def _():
        loop(0, n_hour, lambda k: greet((0, p, k)))

    fill_constants(turn, same_head, pair_sums)

    @pl.when(s == 0)
    def _():
        pl.semaphore_wait(barrier, (n_hour - 1) + (n_patch - 1) + n_hour)

    @pl.when(s == 1)
    def _():
        pl.semaphore_wait(barrier, (n_hour - 1) + (n_patch - 1) + n_patch)

    def send_inputs(m):
        def one(k):
            d = lax.rem(h + k, n_hour)
            remote(
                inputs.at[m, pl.ds(2 * d, 2)],
                timed.at[m, :, at16(h)],
                in_send.at[m, k],
                timed_sem.at[m, h],
                (0, p, d),
            )

        loop(1, n_hour, one)
        pltpu.make_async_copy(
            inputs.at[m, pl.ds(2 * h, 2)], timed.at[m, :, at16(h)], timed_sem.at[m, h]
        ).start()

    @pl.when(s == 0)
    def _():
        send_inputs(0)

    loads[0].wait()
    loads[1].wait()

    def time_step(m):
        loop(0, n_hour, lambda k: arrive(timed.at[m, :, at16(k)], timed_sem.at[m, k]))

        @pl.when((s == 0) & (m == 0))
        def _():
            send_inputs(1)

        x = timed[m].reshape(256, 512)
        y = time_stage(
            x, gains, scales, w_in, w_out, same_head, pair_sums, q_s, ke_s, ko_s, ve_s, vo_s, att_s
        )
        mixed[m] = y.reshape(2, 128, 512)

        def one(k):
            d = lax.rem(h + k, n_hour)
            remote(
                mixed.at[m, :, at16(d)],
                homed.at[m, pl.ds(2 * h, 2)],
                mixed_send.at[m, k],
                homed_sem.at[m, h],
                (s, p, d),
            )

        loop(1, n_hour, one)
        pltpu.make_async_copy(
            mixed.at[m, :, at16(h)], homed.at[m, pl.ds(2 * h, 2)], homed_sem.at[m, h]
        ).start()

    loop(0, 2, time_step)

    def spread_step(m):
        loop(0, n_hour, lambda k: arrive(homed.at[m, pl.ds(2 * k, 2)], homed_sem.at[m, k]))
        turned[m] = dot(turn[...], homed[m].reshape(256, 512)).astype(BF).reshape(16, 16, 512)

        def one(k):
            d = lax.rem(p + k, n_patch)
            remote(
                turned.at[m, d],
                spread.at[m, at16(p)],
                turned_send.at[m, k],
                spread_sem.at[m, p],
                (s, d, h),
            )

        loop(1, n_patch, one)
        pltpu.make_async_copy(turned.at[m, p], spread.at[m, at16(p)], spread_sem.at[m, p]).start()

    loop(0, 2, spread_step)
    loads[2].wait()
    loads[3].wait()

    def patch_step(m):
        loop(0, n_patch, lambda k: arrive(spread.at[m, at16(k)], spread_sem.at[m, k]))
        y = patch_stage(
            spread[m],
            vis,
            gains,
            scales,
            w_in,
            w_out,
            same_head,
            pair_sums,
            q_s,
            ke_s,
            ko_s,
            ve_s,
            vo_s,
            att_s,
        )
        result[m] = feed_forward(y, gains, up, down, hidden)

        def one(k):
            d = lax.rem(p + k, n_patch)
            remote(
                result.at[m, at16(d)],
                back.at[s, m, p],
                result_send.at[m, k],
                back_sem.at[s, m, p],
                (s, d, h),
            )

        loop(1, n_patch, one)
        pltpu.make_async_copy(result.at[m, at16(p)], back.at[s, m, p], back_sem.at[s, m, p]).start()

        @pl.when(s == 1)
        def _():
            def other(k):
                d = lax.rem(p + k, n_patch)
                remote(
                    result.at[m, at16(d)],
                    back.at[1, m, p],
                    final_send.at[m, k],
                    back_sem.at[1, m, p],
                    (0, d, h),
                )

            loop(0, n_patch, other)

    loop(0, 2, patch_step)

    def turn_back(b, m):
        loop(0, n_patch, lambda k: arrive(back.at[b, m, k], back_sem.at[b, m, k]))
        return dot(turn[...], back[b, m].reshape(256, 512)).astype(BF).reshape(16, 16, 512)

    @pl.when(s == 0)
    def _():
        def hand_step(m):
            handed[m] = turn_back(0, m)

            def one(k):
                d = lax.rem(h + k, n_hour)
                remote(
                    handed.at[m, pl.ds(2 * d, 2)],
                    timed.at[m, :, at16(h)],
                    handed_send.at[m, k],
                    timed_sem.at[m, h],
                    (1, p, d),
                )

            loop(0, n_hour, one)

        loop(0, 2, hand_step)

    def final_step(m):
        final[m] = turn_back(1, m)
        pltpu.make_async_copy(final.at[m], out.at[m], out_sem.at[m]).start()

    loop(0, 2, final_step)

    def finish(m):
        def hours(k):
            arrive(mixed.at[m, :, at16(k)], mixed_send.at[m, k])

        def patches(k):
            arrive(turned.at[m, k], turned_send.at[m, k])
            arrive(result.at[m, at16(k)], result_send.at[m, k])

        loop(1, n_hour, hours)
        loop(1, n_patch, patches)

        @pl.when(s == 0)
        def _():
            loop(1, n_hour, lambda k: arrive(timed.at[m, :, at16(k)], in_send.at[m, k]))
            loop(0, n_hour, lambda k: arrive(handed.at[m, pl.ds(2 * k, 2)], handed_send.at[m, k]))

        @pl.when(s == 1)
        def _():
            loop(0, n_patch, lambda k: arrive(result.at[m, at16(k)], final_send.at[m, k]))

        pltpu.make_async_copy(final.at[m], out.at[m], out_sem.at[m]).wait()

    loop(0, 2, finish)


def solution(mesh):
    n_patch, n_hour = mesh.shape["patch"], mesh.shape["hour"]
    placed = (
        P(None, "patch", "hour", None),
        P(),
        P("pipe", None, None),
        P("pipe", None, None),
        P("pipe", None, None, None),
        P("pipe", None, None, None),
        P("pipe", None, None),
        P("pipe", None, None),
    )

    def local(inputs, visibility, norm_gains, scales, mixer_in, mixer_out, expand, reduce):
        tile = (256, 512)
        scratch = [
            pltpu.VMEM((2, 512, 1536), BF),
            pltpu.VMEM((2, 512, 512), BF),
            pltpu.VMEM((512, 2048), BF),
            pltpu.VMEM((2048, 512), BF),
            pltpu.VMEM((2, 2, 128, 512), BF),
            pltpu.VMEM((2, 2, 128, 512), BF),
            pltpu.VMEM((2, 16, 16, 512), BF),
            pltpu.VMEM((2, 16, 16, 512), BF),
            pltpu.VMEM((2, 256, 512), BF),
            pltpu.VMEM((2, 256, 512), BF),
            pltpu.VMEM((2, 2, 16, 16, 512), BF),
            pltpu.VMEM((2, 16, 16, 512), BF),
            pltpu.VMEM((2, 16, 16, 512), BF),
            pltpu.VMEM((256, 256), BF),
            pltpu.VMEM((256, 256), BF),
            pltpu.VMEM((256, 128), BF),
        ]
        scratch += [pltpu.VMEM(tile, BF)]
        scratch += [pltpu.VMEM((4, PB, 512), BF)] * 4
        scratch += [pltpu.VMEM(tile, BF)]
        scratch += [pltpu.VMEM((256, 2048), BF)]
        dma = pltpu.SemaphoreType.DMA
        scratch += [
            dma((4,)),
            dma((2, n_hour)),
            dma((2, n_hour)),
            dma((2, n_patch)),
            dma((2, 2, n_patch)),
            dma((2,)),
            dma((2, n_hour)),
            dma((2, n_hour)),
            dma((2, n_patch)),
            dma((2, n_patch)),
            dma((2, n_patch)),
            dma((2, n_hour)),
        ]
        smem = pl.BlockSpec(memory_space=pltpu.SMEM)
        hbm = pl.BlockSpec(memory_space=pl.ANY)
        return pl.pallas_call(
            functools.partial(kernel, n_patch, n_hour),
            out_shape=jax.ShapeDtypeStruct(inputs.shape, inputs.dtype),
            in_specs=[smem, smem, pl.BlockSpec(memory_space=pltpu.VMEM)] + [hbm] * 5,
            out_specs=hbm,
            scratch_shapes=scratch,
            compiler_params=pltpu.CompilerParams(collective_id=0, has_side_effects=True),
            name="space_time_blocks",
        )(visibility, scales, norm_gains, inputs, mixer_in, mixer_out, expand, reduce)

    return jax.shard_map(
        local, mesh=mesh, in_specs=placed, out_specs=P(None, "patch", "hour", None), check_vma=False
    )
```

time: 455 us -> 109 us (0.24); the launches traced: 446 us -> 109 us
  local copies, waits for them, and re-layouts: 141 us -> 4.51 us
  blocking collectives: 119 us -> 0 us
  Pallas kernels: 0 us -> 104 us
  other arithmetic: 59.4 us -> 0 us
  matrix products: 53.5 us -> 0 us
  waiting for transfers between devices: 47.9 us -> 0 us
  starting transfers between devices: 24.7 us -> 0 us
    all_to_all x9 -> x0, blocking collectives: 119 us -> none  [the longest x3 37.8 us: run_block(): lax.all_to_all(spread, 'patch', split_axis=0, concat_axis=1, tiled=True)]
    pallas_call x0 -> x1, Pallas kernels: none -> 104 us  [local(): pl.pallas_call(functools.partial(kernel, n_patch, n_hour), out_shape=jax....]
    dot_general x30 -> x0, matrix products: 53.5 us -> none  [the longest x3 9.09 us: patch_mix(): jnp.einsum('btnqk,bktnd->bqtnd', weights, value_blocks, preferred_element...]
    gather x12 -> x0, local copies, waits for them, and re-layouts: 40.1 us -> none  [the longest x6 20.1 us: patch_mix(): jnp.take(keys_all.reshape(block_shape), visibility, axis=0)]
    reshape x18 -> x0, local copies, waits for them, and re-layouts: 31.1 us -> none  [the longest x6 12.4 us: split_heads(): keys_all = head_norm(projected[:, width:2 * width].reshape(shape))]
    all_to_all x3 -> x0, waiting for transfers between devices: 26.7 us -> none  [the longest x1 9.22 us: run_block(): lax.all_to_all(hourly, 'hour', split_axis=1, concat_axis=0, tiled=True)]
    all_to_all x3 -> x0, starting transfers between devices: 23.3 us -> none  [the longest x1 10.8 us: run_block(): lax.all_to_all(restored, 'patch', split_axis=1, concat_axis=0, tiled=True)]
    another operation x9 -> x0, local copies, waits for them, and re-layouts: 21.7 us -> none
  transfers between devices with their start and end apart: 6 -> 0, of which waited for: 6 -> 0; matrix products, arithmetic and copies ran while one was open for 0% -> 0% of each run, Pallas kernels for 0% -> 0%
where the time goes in v1:
time: 109 us
  Pallas kernels  104 us (95%)
  local copies, waits for them, and re-layouts  4.51 us (4%)
    pallas_call x1, Pallas kernels, local(): pl.pallas_call(functools.partial(kernel, n_patch, n_hour), out_shape=jax....  104 us
    unnamed x3, local copies, waits for them, and re-layouts  4.51 us

profile of v1, /device:TPU:1, one launch (start us, length us, event | category | flops | bytes accessed | tf_op | source)
XLA Modules:
  0.0 108.9 jit_solution(18265794640051402737)
XLA Ops:
  0.0 1.4 %copy.9.vis = s32[4,2]{1,0:T(4,128)} copy(s32[4,2]{0,1:T(2,128)} %param.9) | data formatting | bytes 64 | tf_op args[1]
  1.4 1.3 %copy.10.gains = f32[1,3,512]{2,1,0:T(4,128)} copy(f32[1,3,512]{2,0,1:T(1,128)} %param.10) | data formatting | bytes 12288 | tf_op args[2]
  2.6 104.4 %space_time_blocks.1 = bf16[2,16,16,512]{3,2,1,0:T(8,128)(2,1)} custom-call(s32[4,2]{1,0:T(4,128)} %copy.9.vis, f32[1,2,8]{2,1,0:T(2,128)} %scales.1, f32[1,3,512]{2,1,0:T(4,128)} %copy.10.gains, bf16[2,16,16,512]{3,2,1,0:T(8,128)(2,1)} %inputs.1, bf16[1,2,512,1536]{3,2,1,0:T(8,128)(2,1)} %w_in_hbm.1, bf16[1,2,512,512]{3,2,1,0:T(8,128)(2,1)} %w_out_hbm.1, ...), custom_call_target="tpu_custom_call" | custom-call | tf_op jit(solution)/shard_map/space_time_blocks/pallas_call | solution.py:460
  107.0 1.9 %copy.12 = bf16[2,16,16,512]{3,2,1,0:T(8,128)(2,1)} copy(bf16[2,16,16,512]{3,2,1,0:T(8,128)(2,1)} %space_time_blocks.1) | data formatting | bytes 1048576

commit v2 on v1

--- a/solution.py
+++ b/solution.py
@@ -79,7 +79,7 @@
 
 
 def time_stage(x, gains, scales, w_in, w_out, same_head, pair_sums, q_s, ke_s, ko_s, ve_s, vo_s, att_s):
-    normed = rms(x, gains[0, 0:1, :])
+    normed = rms(x, gains[0])
     project(normed, 0, w_in, scales, same_head, q_s, ke_s, ko_s, ve_s, vo_s)
     for a in range(2):
         rows = pl.ds(a * 128, 128)
@@ -94,11 +94,11 @@
 def patch_stage(
     x, vis, gains, scales, w_in, w_out, same_head, pair_sums, q_s, ke_s, ko_s, ve_s, vo_s, att_s
 ):
-    normed = rms(x, gains[0, 1:2, :])
+    normed = rms(x, gains[1])
     project(normed, 1, w_in, scales, same_head, q_s, ke_s, ko_s, ve_s, vo_s)
     for b in range(4):
         rows = pl.ds(b * PB, PB)
-        seen = [vis[b, i] for i in range(KV)]
+        seen = [vis[i, b] for i in range(KV)]
         for j in range(4):
             at = pl.ds(j * 128, 128)
             keys = jnp.concatenate([s[z, :, at] for s in (ke_s, ko_s) for z in seen], axis=0)
@@ -108,11 +108,29 @@
 
 
 def feed_forward(x, gains, up, down, hidden):
-    normed = rms(x, gains[0, 2:3, :])
+    normed = rms(x, gains[2])
     for c in range(8):
         at = pl.ds(c * 256, 256)
         hidden[:, at] = gelu(dot(normed, up[:, at])).astype(BF)
     return (x.astype(F32) + dot(hidden[...], down[...])).astype(BF)
+
+
+def hour_order(h, n_hour, with_self):
+    half = n_hour // 2
+    steps = [half] + [k for i in range(half - 1, 0, -1) for k in (i, n_hour - i)] + [0] * with_self
+    return [(k, lax.rem(h + k, n_hour)) for k in steps]
+
+
+def patch_order(p, n_patch, with_self):
+    x, y, c = p // 4, lax.rem(p // 2, 2), lax.rem(p, 2)
+    steps = [(dx, dy, dc) for dy in (1, 0) for dx in (2, 1, 3, 0) for dc in (0, 1)]
+    steps.sort(key=lambda t: (-(min(t[0], 4 - t[0]) + 2 * t[1]), -t[2]))
+    order = []
+    for k, (dx, dy, dc) in enumerate(steps):
+        if (dx, dy, dc) != (0, 0, 0) or with_self:
+            d = lax.rem(x + dx, n_patch // 4) * 4 + lax.rem(y + dy, 2) * 2 + lax.rem(c + dc, 2)
+            order.append((k, d))
+    return order
 
 
 def loop(start, stop, body):
@@ -207,54 +225,49 @@
 
     loop(1, n_hour, lambda k: greet((s, p, lax.rem(h + k, n_hour))))
     loop(1, n_patch, lambda k: greet((s, lax.rem(p + k, n_patch), h)))
+    loop(0, n_hour, lambda k: greet((1 - s, p, k)))
 
     @pl.when(s == 0)
     def _():
         loop(0, n_patch, lambda k: greet((1, k, h)))
 
+    fill_constants(turn, same_head, pair_sums)
+
+    @pl.when(s == 0)
+    def _():
+        pl.semaphore_wait(barrier, (n_hour - 1) + (n_patch - 1) + n_hour)
+
     @pl.when(s == 1)
     def _():
-        loop(0, n_hour, lambda k: greet((0, p, k)))
-
-    fill_constants(turn, same_head, pair_sums)
+        pl.semaphore_wait(barrier, (n_hour - 1) + (n_patch - 1) + n_hour + n_patch)
+
+    def send_input(m, k, d):
+        remote(
+            inputs.at[m, pl.ds(2 * d, 2)],
+            timed.at[m, :, at16(h)],
+            in_send.at[k],
+            timed_sem.at[m, h],
+            (0, p, d),
+        )
 
     @pl.when(s == 0)
     def _():
-        pl.semaphore_wait(barrier, (n_hour - 1) + (n_patch - 1) + n_hour)
+        for k, d in hour_order(h, n_hour, False):
+            send_input(0, k, d)
+        pltpu.make_async_copy(
+            inputs.at[0, pl.ds(2 * h, 2)], timed.at[0, :, at16(h)], timed_sem.at[0, h]
+        ).start()
 
     @pl.when(s == 1)
     def _():
-        pl.semaphore_wait(barrier, (n_hour - 1) + (n_patch - 1) + n_patch)
-
-    def send_inputs(m):
-        def one(k):
-            d = lax.rem(h + k, n_hour)
-            remote(
-                inputs.at[m, pl.ds(2 * d, 2)],
-                timed.at[m, :, at16(h)],
-                in_send.at[m, k],
-                timed_sem.at[m, h],
-                (0, p, d),
-            )
-
-        loop(1, n_hour, one)
-        pltpu.make_async_copy(
-            inputs.at[m, pl.ds(2 * h, 2)], timed.at[m, :, at16(h)], timed_sem.at[m, h]
-        ).start()
-
-    @pl.when(s == 0)
-    def _():
-        send_inputs(0)
+        for k, d in hour_order(h, n_hour, True):
+            send_input(1, k, d)
 
     loads[0].wait()
     loads[1].wait()
 
     def time_step(m):
         loop(0, n_hour, lambda k: arrive(timed.at[m, :, at16(k)], timed_sem.at[m, k]))
-
-        @pl.when((s == 0) & (m == 0))
-        def _():
-            send_inputs(1)
 
         x = timed[m].reshape(256, 512)
         y = time_stage(
@@ -262,8 +275,7 @@
         )
         mixed[m] = y.reshape(2, 128, 512)
 
-        def one(k):
-            d = lax.rem(h + k, n_hour)
+        for k, d in hour_order(h, n_hour, False):
             remote(
                 mixed.at[m, :, at16(d)],
                 homed.at[m, pl.ds(2 * h, 2)],
@@ -271,8 +283,6 @@
                 homed_sem.at[m, h],
                 (s, p, d),
             )
-
-        loop(1, n_hour, one)
         pltpu.make_async_copy(
             mixed.at[m, :, at16(h)], homed.at[m, pl.ds(2 * h, 2)], homed_sem.at[m, h]
         ).start()
@@ -283,8 +293,7 @@
         loop(0, n_hour, lambda k: arrive(homed.at[m, pl.ds(2 * k, 2)], homed_sem.at[m, k]))
         turned[m] = dot(turn[...], homed[m].reshape(256, 512)).astype(BF).reshape(16, 16, 512)
 
-        def one(k):
-            d = lax.rem(p + k, n_patch)
+        for k, d in patch_order(p, n_patch, False):
             remote(
                 turned.at[m, d],
                 spread.at[m, at16(p)],
@@ -292,8 +301,6 @@
                 spread_sem.at[m, p],
                 (s, d, h),
             )
-
-        loop(1, n_patch, one)
         pltpu.make_async_copy(turned.at[m, p], spread.at[m, at16(p)], spread_sem.at[m, p]).start()
 
     loop(0, 2, spread_step)
@@ -320,8 +327,7 @@
         )
         result[m] = feed_forward(y, gains, up, down, hidden)
 
-        def one(k):
-            d = lax.rem(p + k, n_patch)
+        for k, d in patch_order(p, n_patch, False):
             remote(
                 result.at[m, at16(d)],
                 back.at[s, m, p],
@@ -329,14 +335,11 @@
                 back_sem.at[s, m, p],
                 (s, d, h),
             )
-
-        loop(1, n_patch, one)
         pltpu.make_async_copy(result.at[m, at16(p)], back.at[s, m, p], back_sem.at[s, m, p]).start()
 
         @pl.when(s == 1)
         def _():
-            def other(k):
-                d = lax.rem(p + k, n_patch)
+            for k, d in patch_order(p, n_patch, True):
                 remote(
                     result.at[m, at16(d)],
                     back.at[1, m, p],
@@ -345,8 +348,6 @@
                     (0, d, h),
                 )
 
-            loop(0, n_patch, other)
-
     loop(0, 2, patch_step)
 
     def turn_back(b, m):
@@ -358,8 +359,7 @@
         def hand_step(m):
             handed[m] = turn_back(0, m)
 
-            def one(k):
-                d = lax.rem(h + k, n_hour)
+            for k, d in hour_order(h, n_hour, True):
                 remote(
                     handed.at[m, pl.ds(2 * d, 2)],
                     timed.at[m, :, at16(h)],
@@ -368,8 +368,6 @@
                     (1, p, d),
                 )
 
-            loop(0, n_hour, one)
-
         loop(0, 2, hand_step)
 
     def final_step(m):
@@ -387,11 +385,10 @@
             arrive(result.at[m, at16(k)], result_send.at[m, k])
 
         loop(1, n_hour, hours)
-        loop(1, n_patch, patches)
+        loop(0, n_patch - 1, patches)
 
         @pl.when(s == 0)
         def _():
-            loop(1, n_hour, lambda k: arrive(timed.at[m, :, at16(k)], in_send.at[m, k]))
             loop(0, n_hour, lambda k: arrive(handed.at[m, pl.ds(2 * k, 2)], handed_send.at[m, k]))
 
         @pl.when(s == 1)
@@ -401,6 +398,11 @@
         pltpu.make_async_copy(final.at[m], out.at[m], out_sem.at[m]).wait()
 
     loop(0, 2, finish)
+    loop(1, n_hour, lambda k: arrive(timed.at[0, :, at16(k)], in_send.at[k]))
+
+    @pl.when(s == 1)
+    def _():
+        arrive(timed.at[0, :, at16(0)], in_send.at[0])
 
 
 def solution(mesh):
@@ -448,7 +450,7 @@
             dma((2, n_patch)),
             dma((2, 2, n_patch)),
             dma((2,)),
-            dma((2, n_hour)),
+            dma((n_hour,)),
             dma((2, n_hour)),
             dma((2, n_patch)),
             dma((2, n_patch)),
@@ -465,7 +467,16 @@
             scratch_shapes=scratch,
             compiler_params=pltpu.CompilerParams(collective_id=0, has_side_effects=True),
             name="space_time_blocks",
-        )(visibility, scales, norm_gains, inputs, mixer_in, mixer_out, expand, reduce)
+        )(
+            visibility.T,
+            scales,
+            jnp.transpose(norm_gains, (1, 0, 2)),
+            inputs,
+            mixer_in,
+            mixer_out,
+            expand,
+            reduce,
+        )
 
     return jax.shard_map(
         local, mesh=mesh, in_specs=placed, out_specs=P(None, "patch", "hour", None), check_vma=False

time: 109 us -> 98.2 us (0.901)
  Pallas kernels: 104 us -> 96.1 us
  local copies, waits for them, and re-layouts: 4.51 us -> 1.87 us
    pallas_call x1, Pallas kernels: 104 us -> 96.1 us  [local(): pl.pallas_call(functools.partial(kernel, n_patch, n_hour), out_shape=jax....]
    unnamed x3 -> x1, local copies, waits for them, and re-layouts: 4.51 us -> 1.87 us
where the time goes in v2:
time: 98.2 us; the launch traced here: 98 us
  Pallas kernels  96.1 us (98%)
  local copies, waits for them, and re-layouts  1.87 us (2%)
    pallas_call x1, Pallas kernels, local(): pl.pallas_call(functools.partial(kernel, n_patch, n_hour), out_shape=jax....  96.1 us

profile of v2, /device:TPU:1, one launch (start us, length us, event | category | flops | bytes accessed | tf_op | source)
XLA Modules:
  0.0 98.0 jit_solution(2982589906661080411)
XLA Ops:
  0.0 96.1 %space_time_blocks.1 = bf16[2,16,16,512]{3,2,1,0:T(8,128)(2,1)} custom-call(s32[2,4]{1,0:T(2,128)} %bitcast.3, f32[1,2,8]{2,1,0:T(2,128)} %scales.1, f32[3,1,512]{2,1,0:T(1,128)} %bitcast.2, bf16[2,16,16,512]{3,2,1,0:T(8,128)(2,1)} %inputs.1, bf16[1,2,512,1536]{3,2,1,0:T(8,128)(2,1)} %w_in_hbm.1, bf16[1,2,512,512]{3,2,1,0:T(8,128)(2,1)} %w_out_hbm.1, ...), custom_call_target="tpu_custom_call" | custom-call | tf_op jit(solution)/shard_map/space_time_blocks/pallas_call | solution.py:462
  96.1 1.9 %copy.10 = bf16[2,16,16,512]{3,2,1,0:T(8,128)(2,1)} copy(bf16[2,16,16,512]{3,2,1,0:T(8,128)(2,1)} %space_time_blocks.1) | data formatting | bytes 1048576

commit v3 on v2

--- a/solution.py
+++ b/solution.py
@@ -35,9 +35,11 @@
     return (x * factor * gain).astype(BF)
 
 
-def fill_constants(turn, same_head, pair_sums):
+def fill_constants(turn, apart, weave, same_head, pair_sums):
     r, c = iota((256, 256), 0), iota((256, 256), 1)
     turn[...] = jnp.where(c == (r % 16) * 16 + r // 16, 1.0, 0.0).astype(BF)
+    apart[...] = jnp.where(c == 2 * (r % 128) + r // 128, 1.0, 0.0).astype(BF)
+    weave[...] = jnp.where(c == (r % 2) * 128 + r // 2, 1.0, 0.0).astype(BF)
     same_head[...] = jnp.where(r // HEAD_DIM == c // HEAD_DIM, 1.0, 0.0).astype(BF)
     r, c = iota((256, 128), 0), iota((256, 128), 1)
     pair_sums[...] = jnp.where(r // 128 == c // HEAD_DIM, 1.0, 0.0).astype(BF)
@@ -133,6 +135,18 @@
     return order
 
 
+def all_order(p, h, n_patch, n_hour):
+    patches = {}
+    for t in [(dx, dy, dc) for dy in (1, 0) for dx in (2, 1, 3, 0) for dc in (0, 1)]:
+        x, y, c = p // 4, lax.rem(p // 2, 2), lax.rem(p, 2)
+        d = lax.rem(x + t[0], n_patch // 4) * 4 + lax.rem(y + t[1], 2) * 2 + lax.rem(c + t[2], 2)
+        patches[t] = (min(t[0], 4 - t[0]) + 2 * t[1], d)
+    hours = {k: (min(k, n_hour - k), d) for k, d in hour_order(h, n_hour, True)}
+    pairs = [(hops + hop, d, e) for hops, d in patches.values() for hop, e in hours.values()]
+    pairs.sort(key=lambda t: -t[0])
+    return [(d, e) for hops, d, e in pairs if not (d is patches[(0, 0, 0)][1] and e is hours[0][1])]
+
+
 def loop(start, stop, body):
     def step(i, carry):
         body(i)
@@ -158,15 +172,17 @@
     up,
     down,
     timed,
+    arrived,
     mixed,
-    homed,
-    turned,
     spread,
+    handed,
     result,
     back,
-    handed,
     final,
+    x_s,
     turn,
+    apart,
+    weave,
     same_head,
     pair_sums,
     q_s,
@@ -178,16 +194,15 @@
     hidden,
     w_sem,
     timed_sem,
-    homed_sem,
+    arrived_sem,
     spread_sem,
     back_sem,
     out_sem,
     in_send,
     mixed_send,
-    turned_send,
+    handed_send,
     result_send,
     final_send,
-    handed_send,
 ):
     s = lax.axis_index("pipe")
     p = lax.axis_index("patch")
@@ -227,19 +242,11 @@
     loop(1, n_patch, lambda k: greet((s, lax.rem(p + k, n_patch), h)))
     loop(0, n_hour, lambda k: greet((1 - s, p, k)))
 
-    @pl.when(s == 0)
-    def _():
-        loop(0, n_patch, lambda k: greet((1, k, h)))
-
-    fill_constants(turn, same_head, pair_sums)
-
-    @pl.when(s == 0)
-    def _():
-        pl.semaphore_wait(barrier, (n_hour - 1) + (n_patch - 1) + n_hour)
-
-    @pl.when(s == 1)
-    def _():
-        pl.semaphore_wait(barrier, (n_hour - 1) + (n_patch - 1) + n_hour + n_patch)
+    fill_constants(turn, apart, weave, same_head, pair_sums)
+
+    pl.semaphore_wait(barrier, (n_hour - 1) + (n_patch - 1) + n_hour)
+    me = p * n_hour + h
+    hour = h * n_patch + p
 
     def send_input(m, k, d):
         remote(
@@ -267,50 +274,50 @@
     loads[1].wait()
 
     def time_step(m):
-        loop(0, n_hour, lambda k: arrive(timed.at[m, :, at16(k)], timed_sem.at[m, k]))
-
-        x = timed[m].reshape(256, 512)
+        @pl.when(s == 0)
+        def _():
+            loop(0, n_hour, lambda k: arrive(timed.at[m, :, at16(k)], timed_sem.at[m, k]))
+            x_s[...] = timed[m].reshape(256, 512)
+
+        @pl.when(s == 1)
+        def _():
+            arrive(arrived.at[m], arrived_sem.at[m])
+            x_s[...] = dot(apart[...], arrived[m].reshape(256, 512)).astype(BF)
+
         y = time_stage(
-            x, gains, scales, w_in, w_out, same_head, pair_sums, q_s, ke_s, ko_s, ve_s, vo_s, att_s
+            x_s[...],
+            gains,
+            scales,
+            w_in,
+            w_out,
+            same_head,
+            pair_sums,
+            q_s,
+            ke_s,
+            ko_s,
+            ve_s,
+            vo_s,
+            att_s,
         )
-        mixed[m] = y.reshape(2, 128, 512)
-
-        for k, d in hour_order(h, n_hour, False):
+        mixed[m] = dot(weave[...], y).astype(BF).reshape(128, 2, 512)
+        for d, e in all_order(p, h, n_patch, n_hour):
             remote(
-                mixed.at[m, :, at16(d)],
-                homed.at[m, pl.ds(2 * h, 2)],
-                mixed_send.at[m, k],
-                homed_sem.at[m, h],
-                (s, p, d),
+                mixed.at[m, e * n_patch + d],
+                spread.at[m, me],
+                mixed_send.at[m],
+                spread_sem.at[m],
+                (s, d, e),
             )
-        pltpu.make_async_copy(
-            mixed.at[m, :, at16(h)], homed.at[m, pl.ds(2 * h, 2)], homed_sem.at[m, h]
-        ).start()
+        pltpu.make_async_copy(mixed.at[m, hour], spread.at[m, me], spread_sem.at[m]).start()
 
     loop(0, 2, time_step)
-
-    def spread_step(m):
-        loop(0, n_hour, lambda k: arrive(homed.at[m, pl.ds(2 * k, 2)], homed_sem.at[m, k]))
-        turned[m] = dot(turn[...], homed[m].reshape(256, 512)).astype(BF).reshape(16, 16, 512)
-
-        for k, d in patch_order(p, n_patch, False):
-            remote(
-                turned.at[m, d],
-                spread.at[m, at16(p)],
-                turned_send.at[m, k],
-                spread_sem.at[m, p],
-                (s, d, h),
-            )
-        pltpu.make_async_copy(turned.at[m, p], spread.at[m, at16(p)], spread_sem.at[m, p]).start()
-
-    loop(0, 2, spread_step)
     loads[2].wait()
     loads[3].wait()
 
     def patch_step(m):
-        loop(0, n_patch, lambda k: arrive(spread.at[m, at16(k)], spread_sem.at[m, k]))
+        arrive(spread.at[m], spread_sem.at[m])
         y = patch_stage(
-            spread[m],
+            spread[m].reshape(256, 512),
             vis,
             gains,
             scales,
@@ -325,75 +332,57 @@
             vo_s,
             att_s,
         )
-        result[m] = feed_forward(y, gains, up, down, hidden)
-
-        for k, d in patch_order(p, n_patch, False):
-            remote(
-                result.at[m, at16(d)],
-                back.at[s, m, p],
-                result_send.at[m, k],
-                back_sem.at[s, m, p],
-                (s, d, h),
-            )
-        pltpu.make_async_copy(result.at[m, at16(p)], back.at[s, m, p], back_sem.at[s, m, p]).start()
+        x_s[...] = feed_forward(y, gains, up, down, hidden)
+
+        @pl.when(s == 0)
+        def _():
+            handed[m] = x_s[...].reshape(128, 2, 512)
+            for d, e in all_order(p, h, n_patch, n_hour) + [(p, h)]:
+                remote(
+                    handed.at[m, d * n_hour + e],
+                    arrived.at[m, hour],
+                    handed_send.at[m],
+                    arrived_sem.at[m],
+                    (1, d, e),
+                )
 
         @pl.when(s == 1)
         def _():
+            result[m] = x_s[...]
             for k, d in patch_order(p, n_patch, True):
-                remote(
-                    result.at[m, at16(d)],
-                    back.at[1, m, p],
-                    final_send.at[m, k],
-                    back_sem.at[1, m, p],
-                    (0, d, h),
-                )
+                for q in (0, 1):
+                    if q == 0 or k < n_patch - 1:
+                        remote(
+                            result.at[m, at16(d)],
+                            back.at[m, p],
+                            (final_send, result_send)[q].at[m, k],
+                            back_sem.at[m, p],
+                            (q, d, h),
+                        )
+            pltpu.make_async_copy(result.at[m, at16(p)], back.at[m, p], back_sem.at[m, p]).start()
 
     loop(0, 2, patch_step)
 
-    def turn_back(b, m):
-        loop(0, n_patch, lambda k: arrive(back.at[b, m, k], back_sem.at[b, m, k]))
-        return dot(turn[...], back[b, m].reshape(256, 512)).astype(BF).reshape(16, 16, 512)
-
-    @pl.when(s == 0)
-    def _():
-        def hand_step(m):
-            handed[m] = turn_back(0, m)
-
-            for k, d in hour_order(h, n_hour, True):
-                remote(
-                    handed.at[m, pl.ds(2 * d, 2)],
-                    timed.at[m, :, at16(h)],
-                    handed_send.at[m, k],
-                    timed_sem.at[m, h],
-                    (1, p, d),
-                )
-
-        loop(0, 2, hand_step)
-
     def final_step(m):
-        final[m] = turn_back(1, m)
+        loop(0, n_patch, lambda k: arrive(back.at[m, k], back_sem.at[m, k]))
+        turned = dot(turn[...], back[m].reshape(256, 512))
+        final[m] = turned.astype(BF).reshape(16, 16, 512)
         pltpu.make_async_copy(final.at[m], out.at[m], out_sem.at[m]).start()
 
     loop(0, 2, final_step)
 
     def finish(m):
-        def hours(k):
-            arrive(mixed.at[m, :, at16(k)], mixed_send.at[m, k])
-
-        def patches(k):
-            arrive(turned.at[m, k], turned_send.at[m, k])
-            arrive(result.at[m, at16(k)], result_send.at[m, k])
-
-        loop(1, n_hour, hours)
-        loop(0, n_patch - 1, patches)
+        others = pl.ds(0, n_patch * n_hour - 1)
+        arrive(mixed.at[m, others], mixed_send.at[m])
 
         @pl.when(s == 0)
         def _():
-            loop(0, n_hour, lambda k: arrive(handed.at[m, pl.ds(2 * k, 2)], handed_send.at[m, k]))
+            arrive(handed.at[m], handed_send.at[m])
 
         @pl.when(s == 1)
         def _():
             loop(0, n_patch, lambda k: arrive(result.at[m, at16(k)], final_send.at[m, k]))
+            loop(0, n_patch - 1, lambda k: arrive(result.at[m, at16(k)], result_send.at[m, k]))
 
         pltpu.make_async_copy(final.at[m], out.at[m], out_sem.at[m]).wait()
 
@@ -426,14 +415,16 @@
             pltpu.VMEM((512, 2048), BF),
             pltpu.VMEM((2048, 512), BF),
             pltpu.VMEM((2, 2, 128, 512), BF),
-            pltpu.VMEM((2, 2, 128, 512), BF),
+            pltpu.VMEM((2, 128, 2, 512), BF),
+            pltpu.VMEM((2, 128, 2, 512), BF),
+            pltpu.VMEM((2, 128, 2, 512), BF),
+            pltpu.VMEM((2, 128, 2, 512), BF),
+            pltpu.VMEM((2, 256, 512), BF),
             pltpu.VMEM((2, 16, 16, 512), BF),
             pltpu.VMEM((2, 16, 16, 512), BF),
-            pltpu.VMEM((2, 256, 512), BF),
-            pltpu.VMEM((2, 256, 512), BF),
-            pltpu.VMEM((2, 2, 16, 16, 512), BF),
-            pltpu.VMEM((2, 16, 16, 512), BF),
-            pltpu.VMEM((2, 16, 16, 512), BF),
+            pltpu.VMEM(tile, BF),
+            pltpu.VMEM((256, 256), BF),
+            pltpu.VMEM((256, 256), BF),
             pltpu.VMEM((256, 256), BF),
             pltpu.VMEM((256, 256), BF),
             pltpu.VMEM((256, 128), BF),
@@ -446,16 +437,15 @@
         scratch += [
             dma((4,)),
             dma((2, n_hour)),
-            dma((2, n_hour)),
+            dma((2,)),
+            dma((2,)),
             dma((2, n_patch)),
-            dma((2, 2, n_patch)),
             dma((2,)),
             dma((n_hour,)),
-            dma((2, n_hour)),
+            dma((2,)),
+            dma((2,)),
             dma((2, n_patch)),
             dma((2, n_patch)),
-            dma((2, n_patch)),
-            dma((2, n_hour)),
         ]
         smem = pl.BlockSpec(memory_space=pltpu.SMEM)
         hbm = pl.BlockSpec(memory_space=pl.ANY)

time: 98.2 us -> 79.5 us (0.81)
  Pallas kernels: 96.1 us -> 77.4 us
    pallas_call x1, Pallas kernels: 96.1 us -> 77.4 us  [local(): pl.pallas_call(functools.partial(kernel, n_patch, n_hour), out_shape=jax....]
where the time goes in v3:
time: 79.5 us; the launch traced here: 79.3 us
  Pallas kernels  77.4 us (97%)
  local copies, waits for them, and re-layouts  1.87 us (2%)
    pallas_call x1, Pallas kernels, local(): pl.pallas_call(functools.partial(kernel, n_patch, n_hour), out_shape=jax....  77.4 us
    unnamed x1, local copies, waits for them, and re-layouts  1.87 us

profile of v3, /device:TPU:1, one launch (start us, length us, event | category | flops | bytes accessed | tf_op | source)
XLA Modules:
  0.0 79.3 jit_solution(9700048402802740950)
XLA Ops:
  0.0 77.4 %space_time_blocks.1 = bf16[2,16,16,512]{3,2,1,0:T(8,128)(2,1)} custom-call(s32[2,4]{1,0:T(2,128)} %bitcast.3, f32[1,2,8]{2,1,0:T(2,128)} %scales.1, f32[3,1,512]{2,1,0:T(1,128)} %bitcast.2, bf16[2,16,16,512]{3,2,1,0:T(8,128)(2,1)} %inputs.1, bf16[1,2,512,1536]{3,2,1,0:T(8,128)(2,1)} %w_in_hbm.1, bf16[1,2,512,512]{3,2,1,0:T(8,128)(2,1)} %w_out_hbm.1, ...), custom_call_target="tpu_custom_call" | custom-call | tf_op jit(solution)/shard_map/space_time_blocks/pallas_call | solution.py:452
  77.4 1.9 %copy.10 = bf16[2,16,16,512]{3,2,1,0:T(8,128)(2,1)} copy(bf16[2,16,16,512]{3,2,1,0:T(8,128)(2,1)} %space_time_blocks.1) | data formatting | bytes 1048576

commit v4 on v3

--- a/solution.py
+++ b/solution.py
@@ -35,9 +35,8 @@
     return (x * factor * gain).astype(BF)
 
 
-def fill_constants(turn, apart, weave, same_head, pair_sums):
+def fill_constants(apart, weave, same_head, pair_sums):
     r, c = iota((256, 256), 0), iota((256, 256), 1)
-    turn[...] = jnp.where(c == (r % 16) * 16 + r // 16, 1.0, 0.0).astype(BF)
     apart[...] = jnp.where(c == 2 * (r % 128) + r // 128, 1.0, 0.0).astype(BF)
     weave[...] = jnp.where(c == (r % 2) * 128 + r // 2, 1.0, 0.0).astype(BF)
     same_head[...] = jnp.where(r // HEAD_DIM == c // HEAD_DIM, 1.0, 0.0).astype(BF)
@@ -177,10 +176,7 @@
     spread,
     handed,
     result,
-    back,
-    final,
     x_s,
-    turn,
     apart,
     weave,
     same_head,
@@ -197,7 +193,6 @@
     arrived_sem,
     spread_sem,
     back_sem,
-    out_sem,
     in_send,
     mixed_send,
     handed_send,
@@ -242,33 +237,26 @@
     loop(1, n_patch, lambda k: greet((s, lax.rem(p + k, n_patch), h)))
     loop(0, n_hour, lambda k: greet((1 - s, p, k)))
 
-    fill_constants(turn, apart, weave, same_head, pair_sums)
+    fill_constants(apart, weave, same_head, pair_sums)
 
     pl.semaphore_wait(barrier, (n_hour - 1) + (n_patch - 1) + n_hour)
     me = p * n_hour + h
     hour = h * n_patch + p
 
-    def send_input(m, k, d):
-        remote(
-            inputs.at[m, pl.ds(2 * d, 2)],
-            timed.at[m, :, at16(h)],
-            in_send.at[k],
-            timed_sem.at[m, h],
-            (0, p, d),
-        )
-
-    @pl.when(s == 0)
-    def _():
+    for m in range(2):
+        own = (inputs.at[m, 2 * h + s], timed.at[m, s, at16(h)])
         for k, d in hour_order(h, n_hour, False):
-            send_input(0, k, d)
-        pltpu.make_async_copy(
-            inputs.at[0, pl.ds(2 * h, 2)], timed.at[0, :, at16(h)], timed_sem.at[0, h]
-        ).start()
-
-    @pl.when(s == 1)
-    def _():
-        for k, d in hour_order(h, n_hour, True):
-            send_input(1, k, d)
+            remote(
+                inputs.at[m, 2 * d + s], own[1], in_send.at[m, k], timed_sem.at[m, s, h], (0, p, d)
+            )
+
+        @pl.when(s == 0)
+        def _(m=m, own=own):
+            pltpu.make_async_copy(*own, timed_sem.at[m, 0, h]).start()
+
+        @pl.when(s == 1)
+        def _(m=m, own=own):
+            remote(*own, in_send.at[m, 0], timed_sem.at[m, 1, h], (0, p, h))
 
     loads[0].wait()
     loads[1].wait()
@@ -276,7 +264,9 @@
     def time_step(m):
         @pl.when(s == 0)
         def _():
-            loop(0, n_hour, lambda k: arrive(timed.at[m, :, at16(k)], timed_sem.at[m, k]))
+            for a in range(2):
+                loop(0, n_hour, lambda k: arrive(timed.at[m, a, at16(k)], timed_sem.at[m, a, k]))
+
             x_s[...] = timed[m].reshape(256, 512)
 
         @pl.when(s == 1)
@@ -354,26 +344,19 @@
                     if q == 0 or k < n_patch - 1:
                         remote(
                             result.at[m, at16(d)],
-                            back.at[m, p],
+                            out.at[m, p],
                             (final_send, result_send)[q].at[m, k],
                             back_sem.at[m, p],
                             (q, d, h),
                         )
-            pltpu.make_async_copy(result.at[m, at16(p)], back.at[m, p], back_sem.at[m, p]).start()
+            pltpu.make_async_copy(result.at[m, at16(p)], out.at[m, p], back_sem.at[m, p]).start()
 
     loop(0, 2, patch_step)
-
-    def final_step(m):
-        loop(0, n_patch, lambda k: arrive(back.at[m, k], back_sem.at[m, k]))
-        turned = dot(turn[...], back[m].reshape(256, 512))
-        final[m] = turned.astype(BF).reshape(16, 16, 512)
-        pltpu.make_async_copy(final.at[m], out.at[m], out_sem.at[m]).start()
-
-    loop(0, 2, final_step)
 
     def finish(m):
         others = pl.ds(0, n_patch * n_hour - 1)
         arrive(mixed.at[m, others], mixed_send.at[m])
+        loop(1, n_hour, lambda k: arrive(timed.at[0, 0, at16(k)], in_send.at[m, k]))
 
         @pl.when(s == 0)
         def _():
@@ -381,17 +364,13 @@
 
         @pl.when(s == 1)
         def _():
+            arrive(timed.at[0, 0, at16(0)], in_send.at[m, 0])
             loop(0, n_patch, lambda k: arrive(result.at[m, at16(k)], final_send.at[m, k]))
             loop(0, n_patch - 1, lambda k: arrive(result.at[m, at16(k)], result_send.at[m, k]))
 
-        pltpu.make_async_copy(final.at[m], out.at[m], out_sem.at[m]).wait()
+        loop(0, n_patch, lambda k: arrive(out.at[m, k], back_sem.at[m, k]))
 
     loop(0, 2, finish)
-    loop(1, n_hour, lambda k: arrive(timed.at[0, :, at16(k)], in_send.at[k]))
-
-    @pl.when(s == 1)
-    def _():
-        arrive(timed.at[0, :, at16(0)], in_send.at[0])
 
 
 def solution(mesh):
@@ -420,10 +399,7 @@
             pltpu.VMEM((2, 128, 2, 512), BF),
             pltpu.VMEM((2, 128, 2, 512), BF),
             pltpu.VMEM((2, 256, 512), BF),
-            pltpu.VMEM((2, 16, 16, 512), BF),
-            pltpu.VMEM((2, 16, 16, 512), BF),
             pltpu.VMEM(tile, BF),
-            pltpu.VMEM((256, 256), BF),
             pltpu.VMEM((256, 256), BF),
             pltpu.VMEM((256, 256), BF),
             pltpu.VMEM((256, 256), BF),
@@ -436,12 +412,11 @@
         dma = pltpu.SemaphoreType.DMA
         scratch += [
             dma((4,)),
-            dma((2, n_hour)),
+            dma((2, 2, n_hour)),
             dma((2,)),
             dma((2,)),
             dma((2, n_patch)),
-            dma((2,)),
-            dma((n_hour,)),
+            dma((2, n_hour)),
             dma((2,)),
             dma((2,)),
             dma((2, n_patch)),
@@ -449,7 +424,7 @@
         ]
         smem = pl.BlockSpec(memory_space=pltpu.SMEM)
         hbm = pl.BlockSpec(memory_space=pl.ANY)
-        return pl.pallas_call(
+        by_hour = pl.pallas_call(
             functools.partial(kernel, n_patch, n_hour),
             out_shape=jax.ShapeDtypeStruct(inputs.shape, inputs.dtype),
             in_specs=[smem, smem, pl.BlockSpec(memory_space=pltpu.VMEM)] + [hbm] * 5,
@@ -467,6 +442,7 @@
             expand,
             reduce,
         )
+        return jnp.swapaxes(by_hour, 1, 2)
 
     return jax.shard_map(
         local, mesh=mesh, in_specs=placed, out_specs=P(None, "patch", "hour", None), check_vma=False

time: 79.5 us -> 77.1 us (0.970)
  Pallas kernels: 77.4 us -> 74.8 us
    pallas_call x1, Pallas kernels: 77.4 us -> 74.8 us  [local(): pl.pallas_call(functools.partial(kernel, n_patch, n_hour), out_shape=jax....]
    transpose x0 -> x1, local copies, waits for them, and re-layouts: none -> 2.13 us  [local(): return jnp.swapaxes(by_hour, 1, 2)]
    unnamed x1 -> x0, local copies, waits for them, and re-layouts: 1.87 us -> none
where the time goes in v4:
time: 77.1 us; the launch traced here: 76.9 us
  Pallas kernels  74.8 us (97%)
  local copies, waits for them, and re-layouts  2.13 us (3%)
    pallas_call x1, Pallas kernels, local(): pl.pallas_call(functools.partial(kernel, n_patch, n_hour), out_shape=jax....  74.8 us
    transpose x1, local copies, waits for them, and re-layouts, local(): return jnp.swapaxes(by_hour, 1, 2)  2.13 us

profile of v4, /device:TPU:1, one launch (start us, length us, event | category | flops | bytes accessed | tf_op | source)
XLA Modules:
  0.0 76.9 jit_solution(8774619506538753959)
XLA Ops:
  0.0 74.8 %space_time_blocks.1 = bf16[2,16,16,512]{3,2,1,0:T(8,128)(2,1)} custom-call(s32[2,4]{1,0:T(2,128)} %bitcast.5, f32[1,2,8]{2,1,0:T(2,128)} %scales.1, f32[3,1,512]{2,1,0:T(1,128)} %bitcast.4, bf16[2,16,16,512]{3,2,1,0:T(8,128)(2,1)} %inputs.1, bf16[1,2,512,1536]{3,2,1,0:T(8,128)(2,1)} %w_in_hbm.1, bf16[1,2,512,512]{3,2,1,0:T(8,128)(2,1)} %w_out_hbm.1, ...), custom_call_target="tpu_custom_call" | custom-call | tf_op jit(solution)/shard_map/space_time_blocks/pallas_call | solution.py:427
  74.8 2.1 %copy.9 = bf16[2,16,16,512]{3,2,1,0:T(8,128)(2,1)} copy(bf16[2,16,16,512]{3,1,2,0:T(8,128)(2,1)} %bitcast.3) | data formatting | bytes 1048576 | tf_op jit(solution)/shard_map/transpose | solution.py:445

commit v5 on v4

--- a/solution.py
+++ b/solution.py
@@ -39,29 +39,35 @@
     r, c = iota((256, 256), 0), iota((256, 256), 1)
     apart[...] = jnp.where(c == 2 * (r % 128) + r // 128, 1.0, 0.0).astype(BF)
     weave[...] = jnp.where(c == (r % 2) * 128 + r // 2, 1.0, 0.0).astype(BF)
-    same_head[...] = jnp.where(r // HEAD_DIM == c // HEAD_DIM, 1.0, 0.0).astype(BF)
+    same_head[...] = jnp.where(r // HEAD_DIM == c // HEAD_DIM, 1.0 / HEAD_DIM, 0.0).astype(BF)
     r, c = iota((256, 128), 0), iota((256, 128), 1)
     pair_sums[...] = jnp.where(r // 128 == c // HEAD_DIM, 1.0, 0.0).astype(BF)
 
 
-def project(normed, which, weight_in, scales, same_head, q_s, ke_s, ko_s, ve_s, vo_s):
+def project(normed, which, weight_in, scales, same_head, q_s, ke_s, ko_s, ve_s, vo_s, proj_s):
     width = 2 * 256
     lane = iota((1, 256), 1)
     even = (lane // HEAD_DIM) % 2 == 0
     zero = jnp.zeros((256, 256), BF)
+    for part in range(6):
+        proj_s[:, part * 256 : part * 256 + 256] = dot(
+            normed, weight_in[which, :, pl.ds(part * 256, 256)]
+        )
     for part in range(3):
         for half in range(2):
             at = pl.ds(half * 256, 256)
-            value = dot(normed, weight_in[which, :, pl.ds(part * width + half * 256, 256)])
+            value = proj_s[:, pl.ds(part * width + half * 256, 256)]
             if part < 2:
-                squares = dot((value * value).astype(BF), same_head[...])
-                value = value * lax.rsqrt(squares * (1.0 / HEAD_DIM) + 1e-06)
+                square = dot((value * value).astype(BF), same_head[...])
+                value = value * lax.rsqrt(square + 1e-06)
             if part == 0:
                 row = jnp.zeros((1, 256), F32)
                 for n in range(4):
                     scale = scales[0, which, half * 4 + n] * (math.log2(math.e) / HEAD_DIM)
                     row = jnp.where(lane // HEAD_DIM == n, scale, row)
                 q_s[:, at] = (value * row).astype(BF)
+            elif which == 1:
+                (ke_s if part == 1 else ve_s)[:, :, at] = value.astype(BF).reshape(4, PB, 256)
             else:
                 even_s, odd_s = (ke_s, ko_s) if part == 1 else (ve_s, vo_s)
                 value = value.astype(BF)
@@ -69,51 +75,77 @@
                 odd_s[:, :, at] = jnp.where(even, zero, value).reshape(4, PB, 256)
 
 
-def attend(queries, keys, values, pair_sums):
-    weights = jnp.exp2(dot_nt(queries, keys)).astype(BF)
-    mixed = dot(weights, jnp.concatenate([values, pair_sums], axis=1))
-    return (mixed[:, :128] / mixed[:, 128:]).astype(BF)
-
-
-def gelu(u):
-    return 0.5 * u * (1.0 + jnp.tanh(math.sqrt(2.0 / math.pi) * (u + 0.044715 * (u * u * u))))
-
-
-def time_stage(x, gains, scales, w_in, w_out, same_head, pair_sums, q_s, ke_s, ko_s, ve_s, vo_s, att_s):
+def twice_gelu(u):
+    root = math.sqrt(2.0 / math.pi)
+    return u + u * jnp.tanh(u * (root + (root * 0.044715) * (u * u)))
+
+
+def time_stage(x, gains, scales, w_in, w_out, same_head, pair_sums, q_s, ke_s, ko_s, ve_s, vo_s, att_s, proj_s, weigh_s):
     normed = rms(x, gains[0])
-    project(normed, 0, w_in, scales, same_head, q_s, ke_s, ko_s, ve_s, vo_s)
+    project(normed, 0, w_in, scales, same_head, q_s, ke_s, ko_s, ve_s, vo_s, proj_s)
     for a in range(2):
         rows = pl.ds(a * 128, 128)
         for j in range(4):
             at = pl.ds(j * 128, 128)
             keys = jnp.concatenate([k[2 * a + i, :, at] for k in (ke_s, ko_s) for i in range(2)], axis=0)
+            weigh_s[:, pl.ds((a * 4 + j) * 256, 256)] = jnp.exp2(dot_nt(q_s[rows, at], keys)).astype(BF)
+    for a in range(2):
+        rows = pl.ds(a * 128, 128)
+        for j in range(4):
+            at = pl.ds(j * 128, 128)
             values = jnp.concatenate([v[2 * a + i, :, at] for v in (ve_s, vo_s) for i in range(2)], axis=0)
-            att_s[rows, at] = attend(q_s[rows, at], keys, values, pair_sums[...])
+            mixed = dot(
+                weigh_s[:, pl.ds((a * 4 + j) * 256, 256)],
+                jnp.concatenate([values, pair_sums[...]], axis=1),
+            )
+            att_s[rows, at] = (mixed[:, :128] / mixed[:, 128:]).astype(BF)
     return (x.astype(F32) + dot(att_s[...], w_out[0])).astype(BF)
 
 
 def patch_stage(
-    x, vis, gains, scales, w_in, w_out, same_head, pair_sums, q_s, ke_s, ko_s, ve_s, vo_s, att_s
+    x, vis, gains, scales, w_in, w_out, same_head, pair_sums, q_s, ke_s, ko_s, ve_s, vo_s, att_s, proj_s, weigh_s
 ):
     normed = rms(x, gains[1])
-    project(normed, 1, w_in, scales, same_head, q_s, ke_s, ko_s, ve_s, vo_s)
+    project(normed, 1, w_in, scales, same_head, q_s, ke_s, ko_s, ve_s, vo_s, proj_s)
+    even = iota((1, 128), 1) < HEAD_DIM
+    even_pair = iota((1, 256), 1) % 128 < HEAD_DIM
+    zero = jnp.zeros((PB, 128), BF)
+    ones = jnp.ones((128, 128), BF)
     for b in range(4):
         rows = pl.ds(b * PB, PB)
         seen = [vis[i, b] for i in range(KV)]
         for j in range(4):
             at = pl.ds(j * 128, 128)
-            keys = jnp.concatenate([s[z, :, at] for s in (ke_s, ko_s) for z in seen], axis=0)
-            values = jnp.concatenate([s[z, :, at] for s in (ve_s, vo_s) for z in seen], axis=0)
-            att_s[rows, at] = attend(q_s[rows, at], keys, values, pair_sums[...])
+            keys = jnp.concatenate([ke_s[z, :, at] for z in seen], axis=0)
+            queries = q_s[rows, at]
+            queries = jnp.concatenate(
+                [jnp.where(even, queries, zero), jnp.where(even, zero, queries)], axis=0
+            )
+            weigh_s[:, pl.ds((b * 4 + j) * 128, 128)] = jnp.exp2(dot_nt(queries, keys)).astype(BF)
+    for b in range(4):
+        rows = pl.ds(b * PB, PB)
+        seen = [vis[i, b] for i in range(KV)]
+        for j in range(4):
+            at = pl.ds(j * 128, 128)
+            values = jnp.concatenate([ve_s[z, :, at] for z in seen], axis=0)
+            mixed = dot(
+                weigh_s[:, pl.ds((b * 4 + j) * 128, 128)], jnp.concatenate([values, ones], axis=1)
+            )
+            mixed = jnp.where(even_pair, mixed[:PB], mixed[PB:])
+            att_s[rows, at] = (mixed[:, :128] / mixed[:, 128:]).astype(BF)
     return (x.astype(F32) + dot(att_s[...], w_out[1])).astype(BF)
 
 
-def feed_forward(x, gains, up, down, hidden):
+def feed_forward(x, gains, up, down, hidden, proj_s):
     normed = rms(x, gains[2])
-    for c in range(8):
-        at = pl.ds(c * 256, 256)
-        hidden[:, at] = gelu(dot(normed, up[:, at])).astype(BF)
-    return (x.astype(F32) + dot(hidden[...], down[...])).astype(BF)
+    for part in range(2):
+        for c in range(4):
+            at = pl.ds(c * 256, 256)
+            proj_s[:, at] = dot(normed, up[:, pl.ds(part * 1024 + c * 256, 256)])
+        for c in range(4):
+            at = pl.ds(c * 256, 256)
+            hidden[:, pl.ds(part * 1024 + c * 256, 256)] = twice_gelu(proj_s[:, at]).astype(BF)
+    return (x.astype(F32) + 0.5 * dot(hidden[...], down[...])).astype(BF)
 
 
 def hour_order(h, n_hour, with_self):
@@ -187,6 +219,8 @@
     ve_s,
     vo_s,
     att_s,
+    proj_s,
+    weigh_s,
     hidden,
     w_sem,
     timed_sem,
@@ -288,6 +322,8 @@
             ve_s,
             vo_s,
             att_s,
+            proj_s,
+            weigh_s,
         )
         mixed[m] = dot(weave[...], y).astype(BF).reshape(128, 2, 512)
         for d, e in all_order(p, h, n_patch, n_hour):
@@ -321,8 +357,10 @@
             ve_s,
             vo_s,
             att_s,
+            proj_s,
+            weigh_s,
         )
-        x_s[...] = feed_forward(y, gains, up, down, hidden)
+        x_s[...] = feed_forward(y, gains, up, down, hidden, proj_s)
 
         @pl.when(s == 0)
         def _():
@@ -408,6 +446,8 @@
         scratch += [pltpu.VMEM(tile, BF)]
         scratch += [pltpu.VMEM((4, PB, 512), BF)] * 4
         scratch += [pltpu.VMEM(tile, BF)]
+        scratch += [pltpu.VMEM((256, 1536), F32)]
+        scratch += [pltpu.VMEM((128, 2048), BF)]
         scratch += [pltpu.VMEM((256, 2048), BF)]
         dma = pltpu.SemaphoreType.DMA
         scratch += [

time: 77.1 us -> 74.9 us (0.971)
  Pallas kernels: 74.8 us -> 72.6 us
    pallas_call x1, Pallas kernels: 74.8 us -> 72.6 us  [local(): pl.pallas_call(functools.partial(kernel, n_patch, n_hour), out_shape=jax....]
where the time goes in v5:
time: 74.9 us; the launch traced here: 74.7 us
  Pallas kernels  72.6 us (97%)
  local copies, waits for them, and re-layouts  2.13 us (3%)
    pallas_call x1, Pallas kernels, local(): pl.pallas_call(functools.partial(kernel, n_patch, n_hour), out_shape=jax....  72.6 us
    transpose x1, local copies, waits for them, and re-layouts, local(): return jnp.swapaxes(by_hour, 1, 2)  2.13 us

profile of v5, /device:TPU:1, one launch (start us, length us, event | category | flops | bytes accessed | tf_op | source)
XLA Modules:
  0.0 74.7 jit_solution(15526678063540531375)
XLA Ops:
  0.0 72.6 %space_time_blocks.1 = bf16[2,16,16,512]{3,2,1,0:T(8,128)(2,1)} custom-call(s32[2,4]{1,0:T(2,128)} %bitcast.5, f32[1,2,8]{2,1,0:T(2,128)} %scales.1, f32[3,1,512]{2,1,0:T(1,128)} %bitcast.4, bf16[2,16,16,512]{3,2,1,0:T(8,128)(2,1)} %inputs.1, bf16[1,2,512,1536]{3,2,1,0:T(8,128)(2,1)} %w_in_hbm.1, bf16[1,2,512,512]{3,2,1,0:T(8,128)(2,1)} %w_out_hbm.1, ...), custom_call_target="tpu_custom_call" | custom-call | tf_op jit(solution)/shard_map/space_time_blocks/pallas_call | solution.py:467
  72.6 2.1 %copy.9 = bf16[2,16,16,512]{3,2,1,0:T(8,128)(2,1)} copy(bf16[2,16,16,512]{3,1,2,0:T(8,128)(2,1)} %bitcast.3) | data formatting | bytes 1048576 | tf_op jit(solution)/shard_map/transpose | solution.py:485

commit v6 on v5

--- a/solution.py
+++ b/solution.py
@@ -32,7 +32,7 @@
 def rms(x, gain):
     x = x.astype(F32)
     factor = lax.rsqrt(jnp.mean(x * x, axis=-1, keepdims=True) + 1e-05)
-    return (x * factor * gain).astype(BF)
+    return (x * gain).astype(BF), factor
 
 
 def fill_constants(apart, weave, same_head, pair_sums):
@@ -44,35 +44,41 @@
     pair_sums[...] = jnp.where(r // 128 == c // HEAD_DIM, 1.0, 0.0).astype(BF)
 
 
-def project(normed, which, weight_in, scales, same_head, q_s, ke_s, ko_s, ve_s, vo_s, proj_s):
+def project(normed, factor, which, weight_in, scales, same_head, q_s, ke_s, ko_s, ve_s, vo_s, proj_s):
     width = 2 * 256
     lane = iota((1, 256), 1)
     even = (lane // HEAD_DIM) % 2 == 0
     zero = jnp.zeros((256, 256), BF)
-    for part in range(6):
+
+    def put(even_s, odd_s, at, value):
+        value = value.astype(BF)
+        if which == 1:
+            even_s[:, :, at] = value.reshape(4, PB, 256)
+        else:
+            even_s[:, :, at] = jnp.where(even, value, zero).reshape(4, PB, 256)
+            odd_s[:, :, at] = jnp.where(even, zero, value).reshape(4, PB, 256)
+
+    for part in range(4):
         proj_s[:, part * 256 : part * 256 + 256] = dot(
             normed, weight_in[which, :, pl.ds(part * 256, 256)]
         )
-    for part in range(3):
+    for part in range(2):
         for half in range(2):
             at = pl.ds(half * 256, 256)
-            value = proj_s[:, pl.ds(part * width + half * 256, 256)]
-            if part < 2:
-                square = dot((value * value).astype(BF), same_head[...])
-                value = value * lax.rsqrt(square + 1e-06)
+            value = proj_s[:, pl.ds(part * width + half * 256, 256)] * factor
+            square = dot((value * value).astype(BF), same_head[...])
+            value = value * lax.rsqrt(square + 1e-06)
             if part == 0:
                 row = jnp.zeros((1, 256), F32)
                 for n in range(4):
                     scale = scales[0, which, half * 4 + n] * (math.log2(math.e) / HEAD_DIM)
                     row = jnp.where(lane // HEAD_DIM == n, scale, row)
                 q_s[:, at] = (value * row).astype(BF)
-            elif which == 1:
-                (ke_s if part == 1 else ve_s)[:, :, at] = value.astype(BF).reshape(4, PB, 256)
             else:
-                even_s, odd_s = (ke_s, ko_s) if part == 1 else (ve_s, vo_s)
-                value = value.astype(BF)
-                even_s[:, :, at] = jnp.where(even, value, zero).reshape(4, PB, 256)
-                odd_s[:, :, at] = jnp.where(even, zero, value).reshape(4, PB, 256)
+                put(ke_s, ko_s, at, value)
+    for half in range(2):
+        at = pl.ds(half * 256, 256)
+        put(ve_s, vo_s, at, factor * dot(normed, weight_in[which, :, pl.ds(2 * width + half * 256, 256)]))
 
 
 def twice_gelu(u):
@@ -81,8 +87,8 @@
 
 
 def time_stage(x, gains, scales, w_in, w_out, same_head, pair_sums, q_s, ke_s, ko_s, ve_s, vo_s, att_s, proj_s, weigh_s):
-    normed = rms(x, gains[0])
-    project(normed, 0, w_in, scales, same_head, q_s, ke_s, ko_s, ve_s, vo_s, proj_s)
+    normed, factor = rms(x, gains[0])
+    project(normed, factor, 0, w_in, scales, same_head, q_s, ke_s, ko_s, ve_s, vo_s, proj_s)
     for a in range(2):
         rows = pl.ds(a * 128, 128)
         for j in range(4):
@@ -105,8 +111,8 @@
 def patch_stage(
     x, vis, gains, scales, w_in, w_out, same_head, pair_sums, q_s, ke_s, ko_s, ve_s, vo_s, att_s, proj_s, weigh_s
 ):
-    normed = rms(x, gains[1])
-    project(normed, 1, w_in, scales, same_head, q_s, ke_s, ko_s, ve_s, vo_s, proj_s)
+    normed, factor = rms(x, gains[1])
+    project(normed, factor, 1, w_in, scales, same_head, q_s, ke_s, ko_s, ve_s, vo_s, proj_s)
     even = iota((1, 128), 1) < HEAD_DIM
     even_pair = iota((1, 256), 1) % 128 < HEAD_DIM
     zero = jnp.zeros((PB, 128), BF)
@@ -137,14 +143,14 @@
 
 
 def feed_forward(x, gains, up, down, hidden, proj_s):
-    normed = rms(x, gains[2])
+    normed, factor = rms(x, gains[2])
     for part in range(2):
         for c in range(4):
             at = pl.ds(c * 256, 256)
             proj_s[:, at] = dot(normed, up[:, pl.ds(part * 1024 + c * 256, 256)])
         for c in range(4):
             at = pl.ds(c * 256, 256)
-            hidden[:, pl.ds(part * 1024 + c * 256, 256)] = twice_gelu(proj_s[:, at]).astype(BF)
+            hidden[:, pl.ds(part * 1024 + c * 256, 256)] = twice_gelu(proj_s[:, at] * factor).astype(BF)
     return (x.astype(F32) + 0.5 * dot(hidden[...], down[...])).astype(BF)
 
 

time: 74.9 us -> 74.1 us (0.989)
  Pallas kernels: 72.6 us -> 71.8 us
    pallas_call x1, Pallas kernels: 72.6 us -> 71.8 us  [local(): pl.pallas_call(functools.partial(kernel, n_patch, n_hour), out_shape=jax....]
where the time goes in v6:
time: 74.1 us; the launch traced here: 73.9 us
  Pallas kernels  71.8 us (97%)
  local copies, waits for them, and re-layouts  2.13 us (3%)
    pallas_call x1, Pallas kernels, local(): pl.pallas_call(functools.partial(kernel, n_patch, n_hour), out_shape=jax....  71.8 us
    transpose x1, local copies, waits for them, and re-layouts, local(): return jnp.swapaxes(by_hour, 1, 2)  2.13 us

profile of v6, /device:TPU:1, one launch (start us, length us, event | category | flops | bytes accessed | tf_op | source)
XLA Modules:
  0.0 73.9 jit_solution(13381807479414114846)
XLA Ops:
  0.0 71.8 %space_time_blocks.1 = bf16[2,16,16,512]{3,2,1,0:T(8,128)(2,1)} custom-call(s32[2,4]{1,0:T(2,128)} %bitcast.5, f32[1,2,8]{2,1,0:T(2,128)} %scales.1, f32[3,1,512]{2,1,0:T(1,128)} %bitcast.4, bf16[2,16,16,512]{3,2,1,0:T(8,128)(2,1)} %inputs.1, bf16[1,2,512,1536]{3,2,1,0:T(8,128)(2,1)} %w_in_hbm.1, bf16[1,2,512,512]{3,2,1,0:T(8,128)(2,1)} %w_out_hbm.1, ...), custom_call_target="tpu_custom_call" | custom-call | tf_op jit(solution)/shard_map/space_time_blocks/pallas_call | solution.py:473
  71.8 2.1 %copy.9 = bf16[2,16,16,512]{3,2,1,0:T(8,128)(2,1)} copy(bf16[2,16,16,512]{3,1,2,0:T(8,128)(2,1)} %bitcast.3) | data formatting | bytes 1048576 | tf_op jit(solution)/shard_map/transpose | solution.py:491

commit v7 on v6

--- a/solution.py
+++ b/solution.py
@@ -273,9 +273,12 @@
     def greet(device):
         pl.semaphore_signal(barrier, inc=1, device_id=device, device_id_type=MESH)
 
-    loop(1, n_hour, lambda k: greet((s, p, lax.rem(h + k, n_hour))))
-    loop(1, n_patch, lambda k: greet((s, lax.rem(p + k, n_patch), h)))
-    loop(0, n_hour, lambda k: greet((1 - s, p, k)))
+    for k, d in hour_order(h, n_hour, True):
+        greet((1 - s, p, d))
+    for k, d in hour_order(h, n_hour, False):
+        greet((s, p, d))
+    for k, d in patch_order(p, n_patch, False):
+        greet((s, d, h))
 
     fill_constants(apart, weave, same_head, pair_sums)
 
@@ -476,17 +479,19 @@
             in_specs=[smem, smem, pl.BlockSpec(memory_space=pltpu.VMEM)] + [hbm] * 5,
             out_specs=hbm,
             scratch_shapes=scratch,
-            compiler_params=pltpu.CompilerParams(collective_id=0, has_side_effects=True),
+            compiler_params=pltpu.CompilerParams(
+                collective_id=0, has_side_effects=True, vmem_limit_bytes=33554432
+            ),
             name="space_time_blocks",
         )(
-            visibility.T,
-            scales,
-            jnp.transpose(norm_gains, (1, 0, 2)),
-            inputs,
-            mixer_in,
-            mixer_out,
-            expand,
-            reduce,
+            pltpu.with_memory_space_constraint(visibility.T, pltpu.HBM),
+            pltpu.with_memory_space_constraint(scales, pltpu.HBM),
+            pltpu.with_memory_space_constraint(jnp.transpose(norm_gains, (1, 0, 2)), pltpu.HBM),
+            pltpu.with_memory_space_constraint(inputs, pltpu.HBM),
+            pltpu.with_memory_space_constraint(mixer_in, pltpu.HBM),
+            pltpu.with_memory_space_constraint(mixer_out, pltpu.HBM),
+            pltpu.with_memory_space_constraint(expand, pltpu.HBM),
+            pltpu.with_memory_space_constraint(reduce, pltpu.HBM),
         )
         return jnp.swapaxes(by_hour, 1, 2)
 

time: 74.1 us -> 72.7 us (0.981)
  local copies, waits for them, and re-layouts: 2.13 us -> 1.09 us
    transpose x1, local copies, waits for them, and re-layouts: 2.13 us -> 1.09 us  [local(): return jnp.swapaxes(by_hour, 1, 2)]
where the time goes in v7:
time: 72.7 us; the launch traced here: 72.5 us
  Pallas kernels  71.4 us (98%)
  local copies, waits for them, and re-layouts  1.09 us (1%)
    pallas_call x1, Pallas kernels, local(): pl.pallas_call(functools.partial(kernel, n_patch, n_hour), out_shape=jax....  71.4 us

profile of v7, /device:TPU:1, one launch (start us, length us, event | category | flops | bytes accessed | tf_op | source)
XLA Modules:
  0.0 72.5 jit_solution(4496346982602662403)
XLA Ops:
  0.0 71.4 %space_time_blocks.1 = bf16[2,16,16,512]{3,2,1,0:T(8,128)(2,1)S(1)} custom-call(s32[2,4]{1,0:T(2,128)} %bitcast.5, f32[1,2,8]{2,1,0:T(2,128)} %scales.1, f32[3,1,512]{2,1,0:T(1,128)} %bitcast.4, bf16[2,16,16,512]{3,2,1,0:T(8,128)(2,1)} %inputs.1, bf16[1,2,512,1536]{3,2,1,0:T(8,128)(2,1)} %w_in_hbm.1, bf16[1,2,512,512]{3,2,1,0:T(8,128)(2,1)} %w_out_hbm.1, ...), custom_call_target="tpu_custom_call" | custom-call | tf_op jit(solution)/shard_map/space_time_blocks/pallas_call | solution.py:476
  71.4 1.1 %copy.9 = bf16[2,16,16,512]{3,2,1,0:T(8,128)(2,1)} copy(bf16[2,16,16,512]{3,1,2,0:T(8,128)(2,1)S(1)} %bitcast.3) | data formatting | bytes 1048576 | tf_op jit(solution)/shard_map/transpose | solution.py:496
